TPU v7x, 256 devices: a whole 4x4x8 slice. The times are simulated.
256 devices in a mesh: tx: 16 (over z, core), ty: 8 (over x_hi, y), mode: 2 (over x_lo).
Axes of the slice: x: 4 (x_hi: 2, x_lo: 2; x = x_hi * 2 + x_lo), y: 4, z: 8, core: 2. Of those that a mesh axis runs over, the one named last changes fastest.
Arguments:
- obj: float32 [2, 4096, 8192], P(None, 'tx', 'ty'), may hold values from -4 to 4
- probe: float32 [4, 2, 256, 256], P('mode'), may hold values from -4 to 4
- intensity: float32 [16, 8, 2, 256, 256], P('tx', 'ty'), may hold values from 0 to 2
- offsets: int32 [16, 8, 2, 2], P('tx', 'ty'), may hold values from 0 to 1023, as said below
- counts: int32 [16, 8], P('tx', 'ty'), may hold values from 1 to 2, as said below
- patch_filters: float32 [16, 4], replicated, may hold values from -2 to 2
Outputs:
- new_obj: float32 [2, 4096, 8192], P(None, 'tx', 'ty')
Inputs may be any that keep to these rules, and one draw needn't show every extreme that they name: Row offsets are below 256, column offsets below 1024; a pattern may reach into the tiles below and to the right. Slots from counts[a,b] on are empty.
All inputs are finite; a program needn't handle non-finite values.
Results may differ from a plain program's by a relative error of at most 0.00012.
Values sent between devices are 32-bit elements; how exact they have to be, the bound alone decides.
No kernel may reach another device: no remote copies, remote signals or barrier semaphores. Data moves between devices by JAX's collectives and lax.ppermute only.
A program may use at most 128 MiB of HBM per device.

v0:
```python
import functools
import math

import jax
import jax.numpy as jnp
import numpy as np
from jax import lax
from jax.experimental import pallas as pl
from jax.experimental.pallas import tpu as pltpu
from jax.sharding import PartitionSpec as P


W = 256
axes = ("tx", "ty", "mode")
step_size = 0.25
f32 = jnp.float32
bf16 = jnp.bfloat16
VMEM = pl.BlockSpec(memory_space=pltpu.VMEM)
SMEM = pl.BlockSpec(memory_space=pltpu.SMEM)


def rings(mesh):
    n_tx, n_ty = mesh.shape["tx"], mesh.shape["ty"]
    half = n_ty // 2

    def lin(a, b, m):
        return (a * n_ty + b) * 2 + m

    def perm(move):
        return [
            (lin(a, b, m), lin(*move(a, b, m)))
            for a in range(n_tx)
            for b in range(n_ty)
            for m in range(2)
        ]

    def side(b, d, m):
        other = (b + d) % n_ty
        return other, (1 - m if b // half != other // half else m)

    return {
        "up": perm(lambda a, b, m: ((a - 1) % n_tx, b, m)),
        "down": perm(lambda a, b, m: ((a + 1) % n_tx, b, m)),
        "left": perm(lambda a, b, m: (a, *side(b, -1, m))),
        "right": perm(lambda a, b, m: (a, *side(b, 1, m))),
        "core": perm(lambda a, b, m: (a ^ 1, b, m)),
        "swap": perm(lambda a, b, m: (a, b, 1 - m)),
    }


def split(x):
    high = x.astype(bf16)
    return high, (x - high.astype(f32)).astype(bf16)


def tables():
    half = W // 2
    k, l = np.arange(half)[:, None], np.arange(half)[None, :]
    out = []
    for shift in (0, 1):
        angle = (k * (2 * l + shift) % W) * (2.0 * math.pi / W)
        re, im = np.cos(angle) / math.sqrt(W), -np.sin(angle) / math.sqrt(W)
        block = np.block([[re, im], [-im, re]])
        for mat in (block, block.T):
            high = mat.astype(jnp.bfloat16)
            out += [high, (mat - high.astype(np.float64)).astype(jnp.bfloat16)]
    return out


def dot(a, b):
    return jnp.dot(a, b, preferred_element_type=f32)


def rows_times(x, table):
    xh, xl = split(x)
    high, low = table
    return dot(xh, high) + dot(xh, low) + dot(xl, high)


def cols_times(table, x):
    xh, xl = split(x)
    high, low = table
    return dot(high, xh) + dot(low, xh) + dot(high, xl)


def forward(re, im, even, even_t, odd, odd_t):
    h = W // 2

    def lanes(x, y):
        return jnp.concatenate([x, y], axis=1)

    def stack(x, y):
        return jnp.concatenate([x, y], axis=0)

    e = rows_times(lanes(re[:, :h] + re[:, h:], im[:, :h] + im[:, h:]), even)
    o = rows_times(lanes(re[:, :h] - re[:, h:], im[:, :h] - im[:, h:]), odd)
    re, im = lanes(e[:, :h], o[:, :h]), lanes(e[:, h:], o[:, h:])
    e = cols_times(even_t, stack(re[:h] + re[h:], im[:h] + im[h:]))
    o = cols_times(odd_t, stack(re[:h] - re[h:], im[:h] - im[h:]))
    return stack(e[:h], o[:h]), stack(e[h:], o[h:])


def backward(re, im, even, even_t, odd, odd_t):
    h = W // 2

    def lanes(x, y):
        return jnp.concatenate([x, y], axis=1)

    def stack(x, y):
        return jnp.concatenate([x, y], axis=0)

    a = rows_times(lanes(re[:, :h], im[:, :h]), even_t)
    b = rows_times(lanes(re[:, h:], im[:, h:]), odd_t)
    p, n = a + b, a - b
    re, im = lanes(p[:, :h], n[:, :h]), lanes(p[:, h:], n[:, h:])
    a = cols_times(even, stack(re[:h], im[:h]))
    b = cols_times(odd, stack(re[h:], im[h:]))
    p, n = a + b, a - b
    return stack(p[:h], n[:h]), stack(p[h:], n[h:])


def iota(axis):
    return lax.broadcasted_iota(jnp.int32, (W, W), axis)


def window(obj, c, right, q, s):
    lane = iota(1)
    last = lax.axis_index("ty") == lax.axis_size("ty") - 1
    here = obj[c, :, pl.ds(pl.multiple_of(q * W, W), W)]
    nxt = obj[c, :, pl.ds(pl.multiple_of(jnp.minimum(q + 1, 3) * W, W), W)]
    nxt = jnp.where(q == 3, jnp.where(last, 0.0, right[...]), nxt)
    return jnp.where(lane >= s, here, nxt)


def place(table, slot):
    col0 = table[2 * slot + 1]
    return table[2 * slot], col0 // W, lax.rem(col0, W)


def rim_rows(obj, c, row, right, left):
    last = lax.axis_index("ty") == lax.axis_size("ty") - 1
    first = lax.axis_index("ty") == 0
    edge = jnp.where(first, 0.0, left[c, row : row + 1, :])
    parts = [obj[c, row : row + 1, k * W : (k + 1) * W] for k in range(4)]
    parts.append(jnp.where(last, 0.0, right[row : row + 1, :]))
    parts.append(jnp.concatenate([edge, edge], axis=1))
    return parts


def send_body(c, above, obj, left, *refs):
    rights, up_out = refs[: c + 1], refs[c + 1]
    _, q, s = place(above, lax.axis_index("mode"))
    up_out[0:W, :] = window(obj, c, rights[c], q, s)
    for k, part in enumerate(rim_rows(obj, c, 0, rights[c], left)):
        up_out[W + k : W + k + 1, :] = part
    up_out[W + 6 : W + 8, :] = jnp.zeros((2, W), f32)
    if c == 1:
        down_out = refs[c + 2]
        for d in range(2):
            for k, part in enumerate(rim_rows(obj, d, W - 1, rights[d], left)):
                down_out[d, k : k + 1, :] = part
            down_out[d, 6:8, :] = jnp.zeros((2, W), f32)


def main_body(offs, counts, obj, right_0, right_1, below_0, below_1, probe_a, probe_b, probe_c, meas, *refs):
    mats, (grad_0, grad_1, spill_0, spill_1, wave) = refs[:8], refs[8:]
    m = lax.axis_index("mode")
    last_tx = lax.axis_index("tx") == lax.axis_size("tx") - 1
    row0, q, s = place(offs, m)
    live = jnp.where(m < counts[0], 1.0, 0.0).astype(f32)
    lane, row = iota(1), iota(0)
    patch = []
    for c, right, below in ((0, right_0, below_0), (1, right_1, below_1)):
        low = jnp.where(last_tx, 0.0, below[0:W, :])
        rolled = jnp.where(row >= row0, window(obj, c, right, q, s), low)
        rolled = pltpu.roll(rolled, lax.rem(W - row0, W), 0)
        patch.append(pltpu.roll(rolled, lax.rem(W - s, W), 1))

    def probe(k, c):
        return (probe_a[0, c], probe_a[1, c], probe_b[0, c], probe_c[0, c])[k]

    tabs = [(mats[2 * k][...], mats[2 * k + 1][...]) for k in range(4)]
    power = jnp.zeros((W, W), f32)
    for k in range(4):
        pr, pi = probe(k, 0), probe(k, 1)
        wr, wi = forward(pr * patch[0] - pi * patch[1], pr * patch[1] + pi * patch[0], *tabs)
        wave[k, 0] = wr
        wave[k, 1] = wi
        power = power + wr * wr + wi * wi
    resid = power - meas[...]
    grad = [jnp.zeros((W, W), f32), jnp.zeros((W, W), f32)]
    for k in range(4):
        pr, pi = probe(k, 0), probe(k, 1)
        br, bi = backward(resid * wave[k, 0], resid * wave[k, 1], *tabs)
        grad[0] = grad[0] + pr * br + pi * bi
        grad[1] = grad[1] + pr * bi - pi * br
    mark = jnp.where(row >= row0, 1.0, 0.0).astype(f32)
    for g, grad_out, spill_out in ((grad[0], grad_0, spill_0), (grad[1], grad_1, spill_1)):
        g = pltpu.roll(pltpu.roll(g * live, row0, 0), s, 1)
        grad_out[...] = g
        spill_out[...] = jnp.where(lane == W - 1, mark, jnp.where((q == 3) & (lane < s), g, 0.0))


def sort_body(meas, out):
    m = lax.axis_index("mode")
    h = W // 2
    lane, row = iota(1), iota(0)

    def nth(k):
        return jnp.where(k < h, 2 * k, 2 * k - W + 1)

    pick_cols = jnp.where(row == nth(lane), 1.0, 0.0).astype(bf16)
    pick_rows = jnp.where(lane == nth(row), 1.0, 0.0).astype(bf16)

    def parts(x):
        for _ in range(3):
            part = x.astype(bf16)
            x = x - part.astype(f32)
            yield part

    x = sum(dot(part, pick_cols) for part in parts(meas[0, 0, m]))
    out[...] = sum(dot(pick_rows, part) for part in parts(x))


def spill_body(offs, grad, out):
    row0, q, s = place(offs, 1 - lax.axis_index("mode"))
    lane = iota(1)
    mark = jnp.where(iota(0) >= row0, 1.0, 0.0).astype(f32)
    out[...] = jnp.where(lane == W - 1, mark, jnp.where((q == 3) & (lane < s), grad[...], 0.0))


def take(out, c, ref, spot, rows):
    _, q, s = spot
    lane = iota(1)
    value = ref[...]
    here = pl.ds(pl.multiple_of(q * W, W), W)
    out[c, :, here] = out[c, :, here] - step_size * jnp.where(rows & (lane >= s), value, 0.0)
    nxt = pl.ds(pl.multiple_of(jnp.minimum(q + 1, 3) * W, W), W)
    keep = rows & (lane < s) & (q < 3)
    out[c, :, nxt] = out[c, :, nxt] - step_size * jnp.where(keep, value, 0.0)


def prior_body(gram, offs, obj, right_0, right_1, left, up, below_0, below_1, own_0, own_1, out):
    tx, ty = lax.axis_index("tx"), lax.axis_index("ty")
    n_tx, n_ty = lax.axis_size("tx"), lax.axis_size("ty")
    cols = obj.shape[2]
    shape = (W, cols)
    lane = lax.broadcasted_iota(jnp.int32, shape, 1)
    row = lax.broadcasted_iota(jnp.int32, shape, 0)
    g = [[gram[4 * i + j] for j in range(4)] for i in range(4)]

    def beside(x, before, after):
        one_left = jnp.where(lane == 0, before, pltpu.roll(x, 1, 1))
        one_right = jnp.where(lane == cols - 1, after, pltpu.roll(x, cols - 1, 1))
        return one_left, one_right

    spot = place(offs, lax.axis_index("mode"))
    for c, right, below, own in ((0, right_0, below_0, own_0), (1, right_1, below_1, own_1)):
        x = obj[c]
        after = jnp.where(ty == n_ty - 1, 0.0, right[:, 0:1])
        before = jnp.where(ty == 0, 0.0, left[c, :, 127:128])

        def line(rim, flag):
            rim = jnp.where(flag, 0.0, rim)
            whole = jnp.concatenate([rim[k : k + 1, :] for k in range(4)], axis=1)
            return whole, rim[5:6, W - 1 : W], rim[4:5, 0:1]

        u_mid, u_left, u_right = line(up[c], tx == 0)
        d_mid, d_left, d_right = line(below[W : W + 8, :], tx == n_tx - 1)
        xl, xr = beside(x, before, after)

        def above(mid, edge):
            return jnp.where(row == 0, edge, pltpu.roll(mid, 1, 0))

        def under(mid, edge):
            return jnp.where(row == W - 1, edge, pltpu.roll(mid, W - 1, 0))

        def shift_line(mid, b, a):
            l1 = lax.broadcasted_iota(jnp.int32, (1, cols), 1)
            return (
                jnp.where(l1 == 0, b, pltpu.roll(mid, 1, 1)),
                jnp.where(l1 == cols - 1, a, pltpu.roll(mid, cols - 1, 1)),
            )

        ul, ur = shift_line(u_mid, u_left, u_right)
        dl, dr = shift_line(d_mid, d_left, d_right)
        xu, xd = above(x, u_mid), under(x, d_mid)
        xul, xur = above(xl, ul), above(xr, ur)
        xdl, xdr = under(xl, dl), under(xr, dr)
        in_col = (lane > 0) | (ty > 0)
        in_row = (row > 0) | (tx > 0)
        total = g[0][0] * x + g[0][1] * xr + g[0][2] * xd + g[0][3] * xdr
        total += jnp.where(in_col, g[1][0] * xl + g[1][1] * x + g[1][2] * xdl + g[1][3] * xd, 0.0)
        total += jnp.where(in_row, g[2][0] * xu + g[2][1] * xur + g[2][2] * x + g[2][3] * xr, 0.0)
        total += jnp.where(
            in_row & in_col, g[3][0] * xul + g[3][1] * xu + g[3][2] * xl + g[3][3] * x, 0.0
        )
        out[c] = x - step_size * total
        take(out, c, own, spot, iota(0) >= spot[0])


def lower_body(one, two, out):
    first = lax.axis_index("ty") == 0
    lane = iota(1)
    total = jnp.zeros((W, W), f32)
    for ref in (one, two):
        keep = (ref[:, W - 1 : W] < 0.5) & (lane < W - 1)
        total = total + jnp.where(keep, ref[...], 0.0)
    out[...] = jnp.where(first, 0.0, total)


def mid_body(offs, above, base, *refs):
    own_p, left_m, left_p, up_m, up_p = (refs[2 * k : 2 * k + 2] for k in range(5))
    out = refs[10]
    m = lax.axis_index("mode")
    tx, ty = lax.axis_index("tx"), lax.axis_index("ty")
    lane, row = iota(1), iota(0)
    out[...] = base[...]
    mine, from_m, from_p = place(offs, 1 - m), place(above, m), place(above, 1 - m)
    for c in range(2):
        for pair in (left_m, left_p):
            ref = pair[c]
            keep = (ref[:, W - 1 : W] > 0.5) & (lane < W - 1) & (ty > 0)
            out[c, :, 0:W] = out[c, :, 0:W] - step_size * jnp.where(keep, ref[...], 0.0)
        take(out, c, own_p[c], mine, row >= mine[0])
        take(out, c, up_m[c], from_m, (row < from_m[0]) & (tx > 0))
        take(out, c, up_p[c], from_p, (row < from_p[0]) & (tx > 0))


def final_body(mid, corner_0, corner_1, out, buf, sems):
    tx = lax.axis_index("tx")
    loads = [pltpu.make_async_copy(mid.at[c, :, 0:W], buf.at[c], sems.at[c]) for c in range(2)]
    stores = [pltpu.make_async_copy(buf.at[c], out.at[c, :, 0:W], sems.at[2 + c]) for c in range(2)]
    for load in loads:
        load.start()
    for c, corner in enumerate((corner_0, corner_1)):
        loads[c].wait()
        buf[c] = buf[c] - step_size * jnp.where(tx > 0, corner[...], 0.0)
        stores[c].start()
    for store in stores:
        store.wait()


def call(body, shapes, in_specs, limit, flops, bytes_accessed, scratch=(), out_spec=VMEM, aliases={}):
    many = isinstance(shapes, list)
    outs = [jax.ShapeDtypeStruct(s, f32) for s in (shapes if many else [shapes])]
    return pl.pallas_call(
        body,
        out_shape=outs if many else outs[0],
        in_specs=in_specs,
        out_specs=[out_spec] * len(outs) if many else out_spec,
        scratch_shapes=list(scratch),
        input_output_aliases=aliases,
        compiler_params=pltpu.CompilerParams(vmem_limit_bytes=limit << 20),
        cost_estimate=pl.CostEstimate(flops=flops, bytes_accessed=bytes_accessed, transcendentals=0),
    )


def local(ring, obj, probe, intensity, offsets, counts, filters):
    def go(value, where):
        return lax.ppermute(value, axes, ring[where])

    tabs = [jnp.asarray(t) for t in tables()]

    rows, cols = obj.shape[1:]
    piece = (W, W)
    whole = (2, rows, cols)
    offs = offsets.reshape(4)
    live = counts.reshape(1)
    above = go(offs, "down")
    right = [go(obj[c, :, :W], "left") for c in range(2)]
    left = go(obj[:, :, cols - 128 :], "right")
    core = lax.rem(lax.axis_index("tx"), 2)
    probe_b = go(lax.dynamic_slice_in_dim(probe, core, 1, 0), "swap")
    probe_c = go(probe_b, "core")
    gram = jnp.dot(filters.T, filters, precision=lax.Precision.HIGHEST).reshape(16)
    meas = call(sort_body, piece, [VMEM], 8, 1 << 26, 3 << 18)(intensity)
    up_0 = call(
        functools.partial(send_body, 0), (W + 8, W), [SMEM] + [VMEM] * 3, 16, 1 << 20, 2 << 20
    )(above, obj, left, right[0])
    below_0 = go(up_0, "up")
    up_1, rim = call(
        functools.partial(send_body, 1),
        [(W + 8, W), (2, 8, W)],
        [SMEM] + [VMEM] * 4,
        16,
        1 << 20,
        2 << 20,
    )(above, obj, left, *right)
    below_1 = go(up_1, "up")
    over = go(rim, "down")
    below_0, below_1, over = lax.optimization_barrier((below_0, below_1, over))
    g0, g1, s0, s1 = call(
        main_body,
        [piece] * 4,
        [SMEM, SMEM] + [VMEM] * 17,
        16,
        5 << 30,
        12 << 20,
        [pltpu.VMEM((4, 2, W, W), f32)],
    )(offs, live, obj, *right, below_0, below_1, probe, probe_b, probe_c, meas, *tabs)
    p1 = go(g1, "swap")
    m0 = go(s0, "right")
    p0 = go(g0, "swap")
    m1 = go(s1, "right")
    b0, b1 = go(g0, "down"), go(g1, "down")
    base = call(prior_body, whole, [SMEM, SMEM] + [VMEM] * 9, 16, 1 << 28, 16 << 20)(
        gram, offs, obj, *right, left, over, below_0, below_1, g0, g1
    )
    n1 = go(call(spill_body, piece, [SMEM, VMEM], 8, 1 << 18, 1 << 19)(offs, p1), "right")
    n0 = go(m0, "swap")
    c1, c0 = go(p1, "down"), go(p0, "down")
    corner = [
        go(call(lower_body, piece, [VMEM] * 2, 8, 1 << 18, 3 << 18)(a, b), "down")
        for a, b in ((m0, n0), (m1, n1))
    ]
    mid = call(mid_body, whole, [SMEM, SMEM] + [VMEM] * 11, 12, 1 << 24, 10 << 20)(
        offs, above, base, p0, p1, m0, m1, n0, n1, b0, b1, c0, c1
    )
    any_space = pl.BlockSpec(memory_space=pl.ANY)
    return call(
        final_body,
        whole,
        [any_space, VMEM, VMEM],
        8,
        1 << 18,
        2 << 20,
        [pltpu.VMEM((2, W, W), f32), pltpu.SemaphoreType.DMA((4,))],
        any_space,
        {0: 0},
    )(mid, *corner)


def solution(mesh):
    placed = (
        P(None, "tx", "ty"),
        P("mode", None, None, None),
        P("tx", "ty", None, None, None),
        P("tx", "ty", None, None),
        P("tx", "ty"),
        P(),
    )

    def body(*args):
        return local(rings(mesh), *args)

    return jax.shard_map(
        body, mesh=mesh, in_specs=placed, out_specs=P(None, "tx", "ty"), check_vma=False
    )
```

profile of v0, /device:TPU:97, one launch (start us, length us, event | category | flops | bytes accessed | tf_op | source)
XLA Modules:
  0.0 83.5 jit_solution(6356686541112808181)
XLA Ops:
  0.0 1.2 %constant_dynamic-slice_fusion = f32[1,2,256,256]{3,2,1,0:T(8,128)S(1)} fusion(f32[2,2,256,256]{3,2,1,0:T(8,128)} %probe_a.1, s32[]{:T(128)S(6)} %select_n.3), kind=kLoop, calls=%fused_computation.2 | loop fusion | bytes 1048580 | tf_op jit(solution)/shard_map/dynamic_slice | solution.py:374
  1.3 1.3 %collective-permute-start.7 = (f32[1,2,256,256]{3,2,1,0:T(8,128)S(1)}, f32[1,2,256,256]{3,2,1,0:T(8,128)S(1)}, u32[]{:S(2)}, u32[]{:S(2)}) collective-permute-start(f32[1,2,256,256]{3,2,1,0:T(8,128)S(1)} %constant_dynamic-slice_fusion), channel_id=1, source_target_pairs={{0,1},{1,0},{2,3},{3,2},{4,5},{5,4},{6,7},{7,6},{8,9},{9,8},{10,11... | collective-permute-start | bytes 1572872 | tf_op jit(solution)/shard_map/ppermute | solution.py:361
  2.5 1.9 %slice_bitcast_fusion = (f32[256,256]{1,0:T(8,128)}, f32[256,256]{1,0:T(8,128)}) fusion(f32[2,256,1024]{2,1,0:T(8,128)} %obj.7), kind=kLoop, calls=%fused_computation | loop fusion | bytes 1048576 | tf_op jit(solution)/shard_map/squeeze | solution.py:371
  4.4 4.3 %collective-permute-start.1 = (f32[256,256]{1,0:T(8,128)}, f32[256,256]{1,0:T(8,128)S(1)}, u32[]{:S(2)}, u32[]{:S(2)}) collective-permute-start(f32[256,256]{1,0:T(8,128)} %get-tuple-element.24), channel_id=1, source_target_pairs={{0,15},{1,14},{2,0},{3,1},{4,2},{5,3},{6,4},{7,5},{8,7},{9,6},{10,... | collective-permute-start | bytes 786440 | tf_op jit(solution)/shard_map/ppermute | solution.py:361
  8.7 0.7 slice.11
  9.4 4.8 %collective-permute-start.2 = (f32[256,256]{1,0:T(8,128)}, f32[256,256]{1,0:T(8,128)S(1)}, u32[]{:S(2)}, u32[]{:S(2)}) collective-permute-start(f32[256,256]{1,0:T(8,128)} %get-tuple-element.23), channel_id=1, source_target_pairs={{0,15},{1,14},{2,0},{3,1},{4,2},{5,3},{6,4},{7,5},{8,7},{9,6},{10,... | collective-permute-start | bytes 786440 | tf_op jit(solution)/shard_map/ppermute | solution.py:361
  14.2 1.8 %collective-permute-start.8 = (f32[1,2,256,256]{3,2,1,0:T(8,128)S(1)}, f32[1,2,256,256]{3,2,1,0:T(8,128)}, u32[]{:S(2)}, u32[]{:S(2)}) collective-permute-start(f32[1,2,256,256]{3,2,1,0:T(8,128)S(1)} %collective-permute-done.7.probe_b), channel_id=1, source_target_pairs={{0,16},{1,17},{2,18},{3,19},{4,20},{5,21},{6,22},{7,23},{8,24},{9,... | collective-permute-start | bytes 1572872 | tf_op jit(solution)/shard_map/ppermute | solution.py:361
  16.0 0.1 reshape.9.offs
  16.1 2.7 %collective-permute-start = (s32[4]{0:T(128)S(1)}, s32[4]{0:T(128)S(1)}, u32[]{:S(2)}, u32[]{:S(2)}) collective-permute-start(s32[4]{0:T(128)S(1)} %reshape.9.offs), channel_id=1, source_target_pairs={{0,16},{1,17},{2,18},{3,19},{4,20},{5,21},{6,22},{7,23},{8,24},{9,... | collective-permute-start | bytes 56 | tf_op jit(solution)/shard_map/ppermute | solution.py:361
  18.8 0.7 collective-permute-done.above
  19.6 0.0 collective-permute-done.3.left
  19.6 0.6 shard_map.136
  20.2 0.0 copy-start.16
  20.3 2.1 %collective-permute-start.4 = (f32[264,256]{1,0:T(8,128)S(1)}, f32[264,256]{1,0:T(8,128)S(1)}, u32[]{:S(2)}, u32[]{:S(2)}) collective-permute-start(f32[264,256]{1,0:T(8,128)S(1)} %shard_map.136), channel_id=1, source_target_pairs={{0,240},{1,241},{2,242},{3,243},{4,244},{5,245},{6,246},{7,247},{8... | collective-permute-start | bytes 811016 | tf_op jit(solution)/shard_map/ppermute | solution.py:361
  22.4 0.6 shard_map.137
  23.1 0.0 collective-permute-start.5
  23.1 2.9 %collective-permute-start.6 = (f32[2,8,256]{2,1,0:T(8,128)S(1)}, f32[2,8,256]{2,1,0:T(8,128)S(1)}, u32[]{:S(2)}, u32[]{:S(2)}) collective-permute-start(f32[2,8,256]{2,1,0:T(8,128)S(1)} %get-tuple-element.15), channel_id=1, source_target_pairs={{0,16},{1,17},{2,18},{3,19},{4,20},{5,21},{6,22},{7,23},{8,24},{9,... | collective-permute-start | bytes 49160 | tf_op jit(solution)/shard_map/ppermute | solution.py:361
  26.7 0.7 shard_map.138.meas
  27.4 1.9 %collective-permute-done.4.below_0 = f32[264,256]{1,0:T(8,128)S(1)} collective-permute-done((f32[264,256]{1,0:T(8,128)S(1)}, f32[264,256]{1,0:T(8,128)S(1)}, u32[]{:S(2)}, u32[]{:S(2)}) %collective-permute-start.4) | collective-permute-done | bytes 270368 | tf_op jit(solution)/shard_map/ppermute | solution.py:361
  29.3 2.9 %collective-permute-done.5.below_1 = f32[264,256]{1,0:T(8,128)S(1)} collective-permute-done((f32[264,256]{1,0:T(8,128)S(1)}, f32[264,256]{1,0:T(8,128)S(1)}, u32[]{:S(2)}, u32[]{:S(2)}) %collective-permute-start.5) | collective-permute-done | bytes 270368 | tf_op jit(solution)/shard_map/ppermute | solution.py:361
  32.3 8.3 %shard_map.139 = (f32[256,256]{1,0:T(8,128)S(1)}, f32[256,256]{1,0:T(8,128)}, f32[256,256]{1,0:T(8,128)S(1)}, f32[256,256]{1,0:T(8,128)S(1)}) custom-call(s32[4]{0:T(128)S(1)} %reshape.9.offs, s32[1]{0:T(128)} %bitcast.7.counts, f32[2,256,1024]{2,1,0:T(8,128)S(1)} %copy-done.1, f32[256,256]{1,0:T(8,128)S(1)} %collective-permute-done.1.refs_0_.right_0, ...), custom_call_target="tpu_custom_call" | custom-call | flops 5368709120 | bytes 12582912 | tf_op jit(solution)/shard_map/pallas_call | solution.py:393
  40.6 0.1 collective-permute-start.11
  40.7 0.8 collective-permute-start.10
  41.5 0.8 collective-permute-start.9
  42.3 0.8 collective-permute-start.12
  43.1 9.3 %collective-permute-done.11.refs_2_.one = f32[256,256]{1,0:T(8,128)S(1)} collective-permute-done((f32[256,256]{1,0:T(8,128)S(1)}, f32[256,256]{1,0:T(8,128)S(1)}, u32[]{:S(2)}, u32[]{:S(2)}) %collective-permute-start.11) | collective-permute-done | bytes 262176 | tf_op jit(solution)/shard_map/ppermute | solution.py:361
  52.4 1.0 %shard_map.141 = f32[256,256]{1,0:T(8,128)S(1)} custom-call(s32[4]{0:T(128)S(1)} %reshape.9.offs, f32[256,256]{1,0:T(8,128)} %collective-permute-done.10.grad.refs_1_), custom_call_target="tpu_custom_call" | custom-call | flops 262144 | bytes 524288 | tf_op jit(solution)/shard_map/pallas_call | solution.py:410
  53.4 0.1 collective-permute-start.14
  53.5 0.4 collective-permute-start.15
  53.9 0.1 collective-permute-done.9.refs_0_
  54.0 1.5 %collective-permute-start.16 = (f32[256,256]{1,0:T(8,128)}, f32[256,256]{1,0:T(8,128)}, u32[]{:S(2)}, u32[]{:S(2)}) collective-permute-start(f32[256,256]{1,0:T(8,128)} %get-tuple-element.20.own_1), channel_id=1, source_target_pairs={{0,16},{1,17},{2,18},{3,19},{4,20},{5,21},{6,22},{7,23},{8,24},{9,... | collective-permute-start | bytes 786440 | tf_op jit(solution)/shard_map/ppermute | solution.py:361
  55.5 0.2 collective-permute-done.12.refs_3_.one
  55.6 2.7 %collective-permute-start.17 = (f32[256,256]{1,0:T(8,128)}, f32[256,256]{1,0:T(8,128)}, u32[]{:S(2)}, u32[]{:S(2)}) collective-permute-start(f32[256,256]{1,0:T(8,128)} %collective-permute-done.9.refs_0_), channel_id=1, source_target_pairs={{0,16},{1,17},{2,18},{3,19},{4,20},{5,21},{6,22},{7,23},{8,24},{9,... | collective-permute-start | bytes 786440 | tf_op jit(solution)/shard_map/ppermute | solution.py:361
  58.4 3.3 %collective-permute-start.18 = (f32[256,256]{1,0:T(8,128)}, f32[256,256]{1,0:T(8,128)}, u32[]{:S(2)}, u32[]{:S(2)}) collective-permute-start(f32[256,256]{1,0:T(8,128)} %collective-permute-done.10.grad.refs_1_), channel_id=1, source_target_pairs={{0,16},{1,17},{2,18},{3,19},{4,20},{5,21},{6,22},{7,23},{8,24},{9,... | collective-permute-start | bytes 786440 | tf_op jit(solution)/shard_map/ppermute | solution.py:361
  61.7 0.9 %shard_map.143 = f32[256,256]{1,0:T(8,128)} custom-call(f32[256,256]{1,0:T(8,128)S(1)} %collective-permute-done.11.refs_2_.one, f32[256,256]{1,0:T(8,128)S(1)} %collective-permute-done.13.refs_4_.two), custom_call_target="tpu_custom_call" | custom-call | flops 262144 | bytes 786432 | tf_op jit(solution)/shard_map/pallas_call | solution.py:414
  62.5 0.7 copy-done.2
  63.2 2.8 %collective-permute-start.19 = (f32[256,256]{1,0:T(8,128)}, f32[256,256]{1,0:T(8,128)}, u32[]{:S(2)}, u32[]{:S(2)}) collective-permute-start(f32[256,256]{1,0:T(8,128)} %shard_map.143), channel_id=1, source_target_pairs={{0,16},{1,17},{2,18},{3,19},{4,20},{5,21},{6,22},{7,23},{8,24},{9,... | collective-permute-start | bytes 786440 | tf_op jit(solution)/shard_map/ppermute | solution.py:361
  66.1 0.8 %shard_map.144 = f32[256,256]{1,0:T(8,128)} custom-call(f32[256,256]{1,0:T(8,128)S(1)} %collective-permute-done.12.refs_3_.one, f32[256,256]{1,0:T(8,128)S(1)} %collective-permute-done.14.refs_5_.two), custom_call_target="tpu_custom_call" | custom-call | flops 262144 | bytes 786432 | tf_op jit(solution)/shard_map/pallas_call | solution.py:414
  66.9 0.7 copy-done.4
  67.6 0.7 copy-done.13
  68.4 0.1 fusion
  68.5 0.1 reshape.10.gram
  68.6 1.0 %copy-done.8 = f32[264,256]{1,0:T(8,128)S(1)} copy-done((f32[264,256]{1,0:T(8,128)S(1)}, f32[264,256]{1,0:T(8,128)}, u32[]{:S(2)}) %copy-start.8) | copy-done | bytes 270360
  69.5 1.0 %copy-done.10 = f32[264,256]{1,0:T(8,128)S(1)} copy-done((f32[264,256]{1,0:T(8,128)S(1)}, f32[264,256]{1,0:T(8,128)}, u32[]{:S(2)}) %copy-start.10) | copy-done | bytes 270360
  70.5 0.9 %copy-done.12 = f32[256,256]{1,0:T(8,128)S(1)} copy-done((f32[256,256]{1,0:T(8,128)S(1)}, f32[256,256]{1,0:T(8,128)}, u32[]{:S(2)}) %copy-start.12) | copy-done | bytes 262168
  71.4 5.3 %shard_map.140.base = f32[2,256,1024]{2,1,0:T(8,128)S(1)} custom-call(f32[16]{0:T(128)S(1)} %reshape.10.gram, s32[4]{0:T(128)S(1)} %reshape.9.offs, f32[2,256,1024]{2,1,0:T(8,128)S(1)} %copy-done.1, f32[256,256]{1,0:T(8,128)S(1)} %collective-permute-done.1.refs_0_.right_0, f32[256,256]{1,0:T(8,128)S(1)} %collective-permute-done.2.refs_1_.right_1, ...), custom_call_target="tpu_custom_call" | custom-call | flops 268435456 | bytes 16777216 | tf_op jit(solution)/shard_map/pallas_call | solution.py:407
  76.8 3.7 %shard_map.142.mid = f32[2,256,1024]{2,1,0:T(8,128)} custom-call(s32[4]{0:T(128)S(1)} %reshape.9.offs, s32[4]{0:T(128)S(1)} %collective-permute-done.above, f32[2,256,1024]{2,1,0:T(8,128)S(1)} %shard_map.140.base, f32[256,256]{1,0:T(8,128)} %collective-permute-done.9.refs_0_, f32[256,256]{1,0:T(8,128)} %collective-permute-done.10.grad.refs_1_, ...), custom_call_target="tpu_custom_call" | custom-call | flops 16777216 | bytes 10485760 | tf_op jit(solution)/shard_map/pallas_call | solution.py:417
  80.6 2.8 %shard_map.145 = f32[2,256,1024]{2,1,0:T(8,128)} custom-call(f32[2,256,1024]{2,1,0:T(8,128)} %shard_map.142.mid, f32[256,256]{1,0:T(8,128)} %collective-permute-done.19.corner_0, f32[256,256]{1,0:T(8,128)} %collective-permute-done.20.corner_1), custom_call_target="tpu_custom_call", output_to_operand_aliasing={{}: (0, {})} | custom-call | flops 262144 | bytes 2097152 | tf_op jit(solution)/shard_map/pallas_call | solution.py:421
  (60 shorter events, 0.2 us)
Async XLA Ops:
  0.0 68.4 %copy-start = (f32[16,4]{0,1:T(4,128)S(1)}, f32[16,4]{0,1:T(4,128)}, u32[]{:S(2)}) copy-start(f32[16,4]{0,1:T(4,128)} %param.19) | copy-start | bytes 772
  0.0 8.7 %copy-start.1 = (f32[2,256,1024]{2,1,0:T(8,128)S(1)}, f32[2,256,1024]{2,1,0:T(8,128)}, u32[]{:S(2)}) copy-start(f32[2,256,1024]{2,1,0:T(8,128)} %obj.7) | copy-start | bytes 6291460
  0.0 16.0 %copy-start.24 = (s32[1,1,2,2]{3,2,1,0:T(2,128)S(1)}, s32[1,1,2,2]{3,2,1,0:T(2,128)}, u32[]{:S(2)}) copy-start(s32[1,1,2,2]{3,2,1,0:T(2,128)} %param.17) | copy-start | bytes 52
  1.3 13.0 %collective-permute-start.7 = (f32[1,2,256,256]{3,2,1,0:T(8,128)S(1)}, f32[1,2,256,256]{3,2,1,0:T(8,128)S(1)}, u32[]{:S(2)}, u32[]{:S(2)}) collective-permute-start(f32[1,2,256,256]{3,2,1,0:T(8,128)S(1)} %constant_dynamic-slice_fusion), channel_id=1, source_target_pairs={{0,1},{1,0},{2,3},{3,2},{4,5},{5,4},{6,7},{7,6},{8,9},{9,8},{10,11... | collective-permute-start | bytes 1572872 | tf_op jit(solution)/shard_map/ppermute | solution.py:361
  4.4 15.1 %collective-permute-start.1 = (f32[256,256]{1,0:T(8,128)}, f32[256,256]{1,0:T(8,128)S(1)}, u32[]{:S(2)}, u32[]{:S(2)}) collective-permute-start(f32[256,256]{1,0:T(8,128)} %get-tuple-element.24), channel_id=1, source_target_pairs={{0,15},{1,14},{2,0},{3,1},{4,2},{5,3},{6,4},{7,5},{8,7},{9,6},{10,... | collective-permute-start | bytes 786440 | tf_op jit(solution)/shard_map/ppermute | solution.py:361
  9.4 10.2 %collective-permute-start.3 = (f32[2,256,128]{2,1,0:T(8,128)}, f32[2,256,128]{2,1,0:T(8,128)S(1)}, u32[]{:S(2)}, u32[]{:S(2)}) collective-permute-start(f32[2,256,128]{2,1,0:T(8,128)} %slice.11), channel_id=1, source_target_pairs={{0,2},{1,3},{2,4},{3,5},{4,6},{5,7},{6,9},{7,8},{8,10},{9,11},{10,... | collective-permute-start | bytes 786440 | tf_op jit(solution)/shard_map/ppermute | solution.py:361
  9.4 13.0 %collective-permute-start.2 = (f32[256,256]{1,0:T(8,128)}, f32[256,256]{1,0:T(8,128)S(1)}, u32[]{:S(2)}, u32[]{:S(2)}) collective-permute-start(f32[256,256]{1,0:T(8,128)} %get-tuple-element.23), channel_id=1, source_target_pairs={{0,15},{1,14},{2,0},{3,1},{4,2},{5,3},{6,4},{7,5},{8,7},{9,6},{10,... | collective-permute-start | bytes 786440 | tf_op jit(solution)/shard_map/ppermute | solution.py:361
  14.2 18.0 %collective-permute-start.8 = (f32[1,2,256,256]{3,2,1,0:T(8,128)S(1)}, f32[1,2,256,256]{3,2,1,0:T(8,128)}, u32[]{:S(2)}, u32[]{:S(2)}) collective-permute-start(f32[1,2,256,256]{3,2,1,0:T(8,128)S(1)} %collective-permute-done.7.probe_b), channel_id=1, source_target_pairs={{0,16},{1,17},{2,18},{3,19},{4,20},{5,21},{6,22},{7,23},{8,24},{9,... | collective-permute-start | bytes 1572872 | tf_op jit(solution)/shard_map/ppermute | solution.py:361
  16.1 3.5 %collective-permute-start = (s32[4]{0:T(128)S(1)}, s32[4]{0:T(128)S(1)}, u32[]{:S(2)}, u32[]{:S(2)}) collective-permute-start(s32[4]{0:T(128)S(1)} %reshape.9.offs), channel_id=1, source_target_pairs={{0,16},{1,17},{2,18},{3,19},{4,20},{5,21},{6,22},{7,23},{8,24},{9,... | collective-permute-start | bytes 56 | tf_op jit(solution)/shard_map/ppermute | solution.py:361
  20.2 6.5 %copy-start.6 = (f32[1,1,2,256,256]{4,3,2,1,0:T(8,128)S(1)}, f32[1,1,2,256,256]{4,3,2,1,0:T(8,128)}, u32[]{:S(2)}) copy-start(f32[1,1,2,256,256]{4,3,2,1,0:T(8,128)} %meas.1) | copy-start | bytes 1572868
  20.2 12.0 %copy-start.15 = (f32[2,2,256,256]{3,2,1,0:T(8,128)S(1)}, f32[2,2,256,256]{3,2,1,0:T(8,128)}, u32[]{:S(2)}) copy-start(f32[2,2,256,256]{3,2,1,0:T(8,128)} %probe_a.1) | copy-start | bytes 3145732
  20.2 12.0 %copy-start.16 = (bf16[256,256]{1,0:T(8,128)(2,1)S(1)}, bf16[256,256]{1,0:T(8,128)(2,1)}, u32[]{:S(2)}) copy-start(bf16[256,256]{1,0:T(8,128)(2,1)} %constant.28.clone.refs_0_) | copy-start | bytes 393220
  20.3 12.0 %copy-start.17 = (bf16[256,256]{1,0:T(8,128)(2,1)S(1)}, bf16[256,256]{1,0:T(8,128)(2,1)}, u32[]{:S(2)}) copy-start(bf16[256,256]{1,0:T(8,128)(2,1)} %constant.29.clone.refs_1_) | copy-start | bytes 393220
  20.3 12.0 %copy-start.18 = (bf16[256,256]{1,0:T(8,128)(2,1)S(1)}, bf16[256,256]{1,0:T(8,128)(2,1)}, u32[]{:S(2)}) copy-start(bf16[256,256]{1,0:T(8,128)(2,1)} %constant.30.clone.refs_2_) | copy-start | bytes 393220
  20.3 12.0 %copy-start.19 = (bf16[256,256]{1,0:T(8,128)(2,1)S(1)}, bf16[256,256]{1,0:T(8,128)(2,1)}, u32[]{:S(2)}) copy-start(bf16[256,256]{1,0:T(8,128)(2,1)} %constant.31.clone.refs_3_) | copy-start | bytes 393220
  20.3 12.0 %copy-start.20 = (bf16[256,256]{1,0:T(8,128)(2,1)S(1)}, bf16[256,256]{1,0:T(8,128)(2,1)}, u32[]{:S(2)}) copy-start(bf16[256,256]{1,0:T(8,128)(2,1)} %constant.32.clone.refs_4_) | copy-start | bytes 393220
  20.3 12.0 %copy-start.21 = (bf16[256,256]{1,0:T(8,128)(2,1)S(1)}, bf16[256,256]{1,0:T(8,128)(2,1)}, u32[]{:S(2)}) copy-start(bf16[256,256]{1,0:T(8,128)(2,1)} %constant.33.clone.refs_5_) | copy-start | bytes 393220
  20.3 12.0 %copy-start.22 = (bf16[256,256]{1,0:T(8,128)(2,1)S(1)}, bf16[256,256]{1,0:T(8,128)(2,1)}, u32[]{:S(2)}) copy-start(bf16[256,256]{1,0:T(8,128)(2,1)} %constant.34.clone.refs_6_) | copy-start | bytes 393220
  20.3 12.0 %copy-start.23 = (bf16[256,256]{1,0:T(8,128)(2,1)S(1)}, bf16[256,256]{1,0:T(8,128)(2,1)}, u32[]{:S(2)}) copy-start(bf16[256,256]{1,0:T(8,128)(2,1)} %constant.35.clone.refs_7_) | copy-start | bytes 393220
  20.3 9.0 %collective-permute-start.4 = (f32[264,256]{1,0:T(8,128)S(1)}, f32[264,256]{1,0:T(8,128)S(1)}, u32[]{:S(2)}, u32[]{:S(2)}) collective-permute-start(f32[264,256]{1,0:T(8,128)S(1)} %shard_map.136), channel_id=1, source_target_pairs={{0,240},{1,241},{2,242},{3,243},{4,244},{5,245},{6,246},{7,247},{8... | collective-permute-start | bytes 811016 | tf_op jit(solution)/shard_map/ppermute | solution.py:361
  23.1 9.2 %collective-permute-start.5 = (f32[264,256]{1,0:T(8,128)S(1)}, f32[264,256]{1,0:T(8,128)S(1)}, u32[]{:S(2)}, u32[]{:S(2)}) collective-permute-start(f32[264,256]{1,0:T(8,128)S(1)} %get-tuple-element.14), channel_id=1, source_target_pairs={{0,240},{1,241},{2,242},{3,243},{4,244},{5,245},{6,246},{7,247},{8... | collective-permute-start | bytes 811016 | tf_op jit(solution)/shard_map/ppermute | solution.py:361
  23.1 4.3 %collective-permute-start.6 = (f32[2,8,256]{2,1,0:T(8,128)S(1)}, f32[2,8,256]{2,1,0:T(8,128)S(1)}, u32[]{:S(2)}, u32[]{:S(2)}) collective-permute-start(f32[2,8,256]{2,1,0:T(8,128)S(1)} %get-tuple-element.15), channel_id=1, source_target_pairs={{0,16},{1,17},{2,18},{3,19},{4,20},{5,21},{6,22},{7,23},{8,24},{9,... | collective-permute-start | bytes 49160 | tf_op jit(solution)/shard_map/ppermute | solution.py:361
  29.3 11.3 %copy-start.7 = (f32[264,256]{1,0:T(8,128)}, f32[264,256]{1,0:T(8,128)S(1)}, u32[]{:S(2)}) copy-start(f32[264,256]{1,0:T(8,128)S(1)} %collective-permute-done.4.below_0) | copy-start | bytes 811012
  32.2 8.4 %copy-start.9 = (f32[264,256]{1,0:T(8,128)}, f32[264,256]{1,0:T(8,128)S(1)}, u32[]{:S(2)}) copy-start(f32[264,256]{1,0:T(8,128)S(1)} %collective-permute-done.5.below_1) | copy-start | bytes 811012
  40.6 26.3 %copy-start.11 = (f32[256,256]{1,0:T(8,128)}, f32[256,256]{1,0:T(8,128)S(1)}, u32[]{:S(2)}) copy-start(f32[256,256]{1,0:T(8,128)S(1)} %get-tuple-element.19.own_0) | copy-start | bytes 786436
  40.6 11.7 %collective-permute-start.11 = (f32[256,256]{1,0:T(8,128)S(1)}, f32[256,256]{1,0:T(8,128)S(1)}, u32[]{:S(2)}, u32[]{:S(2)}) collective-permute-start(f32[256,256]{1,0:T(8,128)S(1)} %get-tuple-element.21), channel_id=1, source_target_pairs={{0,2},{1,3},{2,4},{3,5},{4,6},{5,7},{6,9},{7,8},{8,10},{9,11},{10,... | collective-permute-start | bytes 786440 | tf_op jit(solution)/shard_map/ppermute | solution.py:361
  40.7 11.6 %collective-permute-start.10 = (f32[256,256]{1,0:T(8,128)}, f32[256,256]{1,0:T(8,128)}, u32[]{:S(2)}, u32[]{:S(2)}) collective-permute-start(f32[256,256]{1,0:T(8,128)} %get-tuple-element.20.own_1), channel_id=1, source_target_pairs={{0,1},{1,0},{2,3},{3,2},{4,5},{5,4},{6,7},{7,6},{8,9},{9,8},{10,11... | collective-permute-start | bytes 786440 | tf_op jit(solution)/shard_map/ppermute | solution.py:361
  41.5 12.5 %collective-permute-start.9 = (f32[256,256]{1,0:T(8,128)S(1)}, f32[256,256]{1,0:T(8,128)}, u32[]{:S(2)}, u32[]{:S(2)}) collective-permute-start(f32[256,256]{1,0:T(8,128)S(1)} %get-tuple-element.19.own_0), channel_id=1, source_target_pairs={{0,1},{1,0},{2,3},{3,2},{4,5},{5,4},{6,7},{7,6},{8,9},{9,8},{10,11... | collective-permute-start | bytes 786440 | tf_op jit(solution)/shard_map/ppermute | solution.py:361
  42.3 13.3 %collective-permute-start.12 = (f32[256,256]{1,0:T(8,128)S(1)}, f32[256,256]{1,0:T(8,128)S(1)}, u32[]{:S(2)}, u32[]{:S(2)}) collective-permute-start(f32[256,256]{1,0:T(8,128)S(1)} %get-tuple-element.22), channel_id=1, source_target_pairs={{0,2},{1,3},{2,4},{3,5},{4,6},{5,7},{6,9},{7,8},{8,10},{9,11},{10,... | collective-permute-start | bytes 786440 | tf_op jit(solution)/shard_map/ppermute | solution.py:361
  52.4 6.0 %collective-permute-start.13 = (f32[256,256]{1,0:T(8,128)S(1)}, f32[256,256]{1,0:T(8,128)S(1)}, u32[]{:S(2)}, u32[]{:S(2)}) collective-permute-start(f32[256,256]{1,0:T(8,128)S(1)} %collective-permute-done.11.refs_2_.one), channel_id=1, source_target_pairs={{0,1},{1,0},{2,3},{3,2},{4,5},{5,4},{6,7},{7,6},{8,9},{9,8},{10,11... | collective-permute-start | bytes 786440 | tf_op jit(solution)/shard_map/ppermute | solution.py:361
  53.4 9.9 %collective-permute-start.14 = (f32[256,256]{1,0:T(8,128)S(1)}, f32[256,256]{1,0:T(8,128)S(1)}, u32[]{:S(2)}, u32[]{:S(2)}) collective-permute-start(f32[256,256]{1,0:T(8,128)S(1)} %shard_map.141), channel_id=1, source_target_pairs={{0,2},{1,3},{2,4},{3,5},{4,6},{5,7},{6,9},{7,8},{8,10},{9,11},{10,... | collective-permute-start | bytes 786440 | tf_op jit(solution)/shard_map/ppermute | solution.py:361
  53.5 14.2 %collective-permute-start.15 = (f32[256,256]{1,0:T(8,128)S(1)}, f32[256,256]{1,0:T(8,128)S(1)}, u32[]{:S(2)}, u32[]{:S(2)}) collective-permute-start(f32[256,256]{1,0:T(8,128)S(1)} %get-tuple-element.19.own_0), channel_id=1, source_target_pairs={{0,16},{1,17},{2,18},{3,19},{4,20},{5,21},{6,22},{7,23},{8,24},{9,... | collective-permute-start | bytes 786440 | tf_op jit(solution)/shard_map/ppermute | solution.py:361
  54.0 22.7 %collective-permute-start.16 = (f32[256,256]{1,0:T(8,128)}, f32[256,256]{1,0:T(8,128)}, u32[]{:S(2)}, u32[]{:S(2)}) collective-permute-start(f32[256,256]{1,0:T(8,128)} %get-tuple-element.20.own_1), channel_id=1, source_target_pairs={{0,16},{1,17},{2,18},{3,19},{4,20},{5,21},{6,22},{7,23},{8,24},{9,... | collective-permute-start | bytes 786440 | tf_op jit(solution)/shard_map/ppermute | solution.py:361
  55.6 21.1 %collective-permute-start.17 = (f32[256,256]{1,0:T(8,128)}, f32[256,256]{1,0:T(8,128)}, u32[]{:S(2)}, u32[]{:S(2)}) collective-permute-start(f32[256,256]{1,0:T(8,128)} %collective-permute-done.9.refs_0_), channel_id=1, source_target_pairs={{0,16},{1,17},{2,18},{3,19},{4,20},{5,21},{6,22},{7,23},{8,24},{9,... | collective-permute-start | bytes 786440 | tf_op jit(solution)/shard_map/ppermute | solution.py:361
  58.4 18.4 %collective-permute-start.18 = (f32[256,256]{1,0:T(8,128)}, f32[256,256]{1,0:T(8,128)}, u32[]{:S(2)}, u32[]{:S(2)}) collective-permute-start(f32[256,256]{1,0:T(8,128)} %collective-permute-done.10.grad.refs_1_), channel_id=1, source_target_pairs={{0,16},{1,17},{2,18},{3,19},{4,20},{5,21},{6,22},{7,23},{8,24},{9,... | collective-permute-start | bytes 786440 | tf_op jit(solution)/shard_map/ppermute | solution.py:361
  62.5 0.7 copy-start.2
  63.2 17.3 %collective-permute-start.19 = (f32[256,256]{1,0:T(8,128)}, f32[256,256]{1,0:T(8,128)}, u32[]{:S(2)}, u32[]{:S(2)}) collective-permute-start(f32[256,256]{1,0:T(8,128)} %shard_map.143), channel_id=1, source_target_pairs={{0,16},{1,17},{2,18},{3,19},{4,20},{5,21},{6,22},{7,23},{8,24},{9,... | collective-permute-start | bytes 786440 | tf_op jit(solution)/shard_map/ppermute | solution.py:361
  66.9 0.7 copy-start.4
  67.6 0.7 copy-start.13
  68.4 12.2 %collective-permute-start.20 = (f32[256,256]{1,0:T(8,128)}, f32[256,256]{1,0:T(8,128)}, u32[]{:S(2)}, u32[]{:S(2)}) collective-permute-start(f32[256,256]{1,0:T(8,128)} %shard_map.144), channel_id=1, source_target_pairs={{0,16},{1,17},{2,18},{3,19},{4,20},{5,21},{6,22},{7,23},{8,24},{9,... | collective-permute-start | bytes 786440 | tf_op jit(solution)/shard_map/ppermute | solution.py:361
  68.6 1.0 %copy-start.8 = (f32[264,256]{1,0:T(8,128)S(1)}, f32[264,256]{1,0:T(8,128)}, u32[]{:S(2)}) copy-start(f32[264,256]{1,0:T(8,128)} %copy-done.7) | copy-start | bytes 811012
  69.5 1.0 %copy-start.10 = (f32[264,256]{1,0:T(8,128)S(1)}, f32[264,256]{1,0:T(8,128)}, u32[]{:S(2)}) copy-start(f32[264,256]{1,0:T(8,128)} %copy-done.9) | copy-start | bytes 811012
  70.5 0.9 %copy-start.12 = (f32[256,256]{1,0:T(8,128)S(1)}, f32[256,256]{1,0:T(8,128)}, u32[]{:S(2)}) copy-start(f32[256,256]{1,0:T(8,128)} %copy-done.11) | copy-start | bytes 786436
  71.4 5.3 %copy-start.3 = (f32[256,256]{1,0:T(8,128)S(1)}, f32[256,256]{1,0:T(8,128)}, u32[]{:S(2)}) copy-start(f32[256,256]{1,0:T(8,128)} %copy-done.2) | copy-start | bytes 786436
  71.4 5.4 %copy-start.5 = (f32[256,256]{1,0:T(8,128)S(1)}, f32[256,256]{1,0:T(8,128)}, u32[]{:S(2)}) copy-start(f32[256,256]{1,0:T(8,128)} %copy-done.4) | copy-start | bytes 786436
  71.4 5.4 %copy-start.14 = (f32[256,256]{1,0:T(8,128)S(1)}, f32[256,256]{1,0:T(8,128)}, u32[]{:S(2)}) copy-start(f32[256,256]{1,0:T(8,128)} %copy-done.13) | copy-start | bytes 786436
where the time goes:
time: 83.9 us; the launch traced here: 83.5 us
  starting transfers between devices  33.2 us (40%)
  Pallas kernels  24.8 us (30%)
  waiting for transfers between devices  15.2 us (18%)
  local copies, waits for them, and re-layouts  9.08 us (11%)
  between operations  1.12 us (1%)
    ppermute x21, starting transfers between devices, go(): return lax.ppermute(value, axes, ring[where])  33.2 us
    ppermute x21, waiting for transfers between devices, go(): return lax.ppermute(value, axes, ring[where])  15.2 us
    pallas_call x1, Pallas kernels, local(): call(main_body, [piece] * 4, [SMEM, SMEM] + [VMEM] * 17, 16, 5 << 30, 12...  8.32 us
    pallas_call x1, Pallas kernels, local(): call(prior_body, whole, [SMEM, SMEM] + [VMEM] * 9, 16, 1 << 28, 16 << 20)  5.3 us
    unnamed x50, local copies, waits for them, and re-layouts  5.07 us
    pallas_call x1, Pallas kernels, local(): call(mid_body, whole, [SMEM, SMEM] + [VMEM] * 11, 12, 1 << 24, 10 << 20)  3.73 us
    pallas_call x1, Pallas kernels, local(): call(final_body, whole, [any_space, VMEM, VMEM], 8, 1 << 18, 2 << 20, [pl...  2.83 us
    squeeze x1, local copies, waits for them, and re-layouts, local(): right = [go(obj[c, :, :W], 'left') for c in range(2)]  1.88 us
  transfers between devices with their start and end apart: 21, of which 6 were waited for; matrix products, arithmetic and copies ran while one was open for 3% of the time, Pallas kernels for 16%

commit v1 on v0

--- a/solution.py
+++ b/solution.py
@@ -133,8 +133,8 @@
 
 
 def place(table, slot):
-    col0 = table[2 * slot + 1]
-    return table[2 * slot], col0 // W, lax.rem(col0, W)
+    col0 = table[slot, 1]
+    return table[slot, 0], col0 // W, lax.rem(col0, W)
 
 
 def rim_rows(obj, c, row, right, left):
@@ -147,31 +147,29 @@
     return parts
 
 
-def send_body(c, above, obj, left, *refs):
-    rights, up_out = refs[: c + 1], refs[c + 1]
+def send_body(c, above, obj, right, out):
     _, q, s = place(above, lax.axis_index("mode"))
-    up_out[0:W, :] = window(obj, c, rights[c], q, s)
-    for k, part in enumerate(rim_rows(obj, c, 0, rights[c], left)):
-        up_out[W + k : W + k + 1, :] = part
-    up_out[W + 6 : W + 8, :] = jnp.zeros((2, W), f32)
-    if c == 1:
-        down_out = refs[c + 2]
-        for d in range(2):
-            for k, part in enumerate(rim_rows(obj, d, W - 1, rights[d], left)):
-                down_out[d, k : k + 1, :] = part
-            down_out[d, 6:8, :] = jnp.zeros((2, W), f32)
+    out[...] = window(obj, c, right, q, s)
+
+
+def rim_body(obj, left, right_0, right_1, up_out, down_out):
+    for c, right in enumerate((right_0, right_1)):
+        for row, out in ((0, up_out), (W - 1, down_out)):
+            for k, part in enumerate(rim_rows(obj, c, row, right, left)):
+                out[c, k : k + 1, :] = part
+            out[c, 6:8, :] = jnp.zeros((2, W), f32)
 
 
 def main_body(offs, counts, obj, right_0, right_1, below_0, below_1, probe_a, probe_b, probe_c, meas, *refs):
-    mats, (grad_0, grad_1, spill_0, spill_1, wave) = refs[:8], refs[8:]
+    mats, (grad_0, grad_1, spill_0, spill_1, keep_0, keep_1, wave) = refs[:8], refs[8:]
     m = lax.axis_index("mode")
     last_tx = lax.axis_index("tx") == lax.axis_size("tx") - 1
     row0, q, s = place(offs, m)
-    live = jnp.where(m < counts[0], 1.0, 0.0).astype(f32)
+    live = jnp.where(m < counts[0, 0], 1.0, 0.0).astype(f32)
     lane, row = iota(1), iota(0)
     patch = []
     for c, right, below in ((0, right_0, below_0), (1, right_1, below_1)):
-        low = jnp.where(last_tx, 0.0, below[0:W, :])
+        low = jnp.where(last_tx, 0.0, below[...])
         rolled = jnp.where(row >= row0, window(obj, c, right, q, s), low)
         rolled = pltpu.roll(rolled, lax.rem(W - row0, W), 0)
         patch.append(pltpu.roll(rolled, lax.rem(W - s, W), 1))
@@ -195,9 +193,13 @@
         grad[0] = grad[0] + pr * br + pi * bi
         grad[1] = grad[1] + pr * bi - pi * br
     mark = jnp.where(row >= row0, 1.0, 0.0).astype(f32)
-    for g, grad_out, spill_out in ((grad[0], grad_0, spill_0), (grad[1], grad_1, spill_1)):
+    for g, grad_out, spill_out, keep_out in (
+        (grad[0], grad_0, spill_0, keep_0),
+        (grad[1], grad_1, spill_1, keep_1),
+    ):
         g = pltpu.roll(pltpu.roll(g * live, row0, 0), s, 1)
         grad_out[...] = g
+        keep_out[...] = g
         spill_out[...] = jnp.where(lane == W - 1, mark, jnp.where((q == 3) & (lane < s), g, 0.0))
 
 
@@ -240,14 +242,15 @@
     out[c, :, nxt] = out[c, :, nxt] - step_size * jnp.where(keep, value, 0.0)
 
 
-def prior_body(gram, offs, obj, right_0, right_1, left, up, below_0, below_1, own_0, own_1, out):
+def prior_body(filt, offs, obj, right_0, right_1, left, up, down, own_0, own_1, out):
     tx, ty = lax.axis_index("tx"), lax.axis_index("ty")
     n_tx, n_ty = lax.axis_size("tx"), lax.axis_size("ty")
     cols = obj.shape[2]
     shape = (W, cols)
     lane = lax.broadcasted_iota(jnp.int32, shape, 1)
     row = lax.broadcasted_iota(jnp.int32, shape, 0)
-    g = [[gram[4 * i + j] for j in range(4)] for i in range(4)]
+    taps = [[filt[i, k] for i in range(4)] for k in range(filt.shape[1])]
+    g = [[sum(tap[i] * tap[j] for tap in taps) for j in range(4)] for i in range(4)]
 
     def beside(x, before, after):
         one_left = jnp.where(lane == 0, before, pltpu.roll(x, 1, 1))
@@ -255,7 +258,7 @@
         return one_left, one_right
 
     spot = place(offs, lax.axis_index("mode"))
-    for c, right, below, own in ((0, right_0, below_0, own_0), (1, right_1, below_1, own_1)):
+    for c, right, own in ((0, right_0, own_0), (1, right_1, own_1)):
         x = obj[c]
         after = jnp.where(ty == n_ty - 1, 0.0, right[:, 0:1])
         before = jnp.where(ty == 0, 0.0, left[c, :, 127:128])
@@ -266,7 +269,7 @@
             return whole, rim[5:6, W - 1 : W], rim[4:5, 0:1]
 
         u_mid, u_left, u_right = line(up[c], tx == 0)
-        d_mid, d_left, d_right = line(below[W : W + 8, :], tx == n_tx - 1)
+        d_mid, d_left, d_right = line(down[c], tx == n_tx - 1)
         xl, xr = beside(x, before, after)
 
         def above(mid, edge):
@@ -365,47 +368,43 @@
     rows, cols = obj.shape[1:]
     piece = (W, W)
     whole = (2, rows, cols)
-    offs = offsets.reshape(4)
-    live = counts.reshape(1)
-    above = go(offs, "down")
-    right = [go(obj[c, :, :W], "left") for c in range(2)]
-    left = go(obj[:, :, cols - 128 :], "right")
+    offs = offsets.reshape(2, 2)
+    right = [go(obj[0, :, :W], "left")]
+    right.append(go(lax.optimization_barrier(obj)[1, :, :W], "left"))
     core = lax.rem(lax.axis_index("tx"), 2)
     probe_b = go(lax.dynamic_slice_in_dim(probe, core, 1, 0), "swap")
     probe_c = go(probe_b, "core")
-    gram = jnp.dot(filters.T, filters, precision=lax.Precision.HIGHEST).reshape(16)
+    above = go(offs, "down")
+    left = go(obj[:, :, cols - 128 :], "right")
+    filt = filters.T
     meas = call(sort_body, piece, [VMEM], 8, 1 << 26, 3 << 18)(intensity)
-    up_0 = call(
-        functools.partial(send_body, 0), (W + 8, W), [SMEM] + [VMEM] * 3, 16, 1 << 20, 2 << 20
-    )(above, obj, left, right[0])
-    below_0 = go(up_0, "up")
-    up_1, rim = call(
-        functools.partial(send_body, 1),
-        [(W + 8, W), (2, 8, W)],
-        [SMEM] + [VMEM] * 4,
-        16,
-        1 << 20,
-        2 << 20,
-    )(above, obj, left, *right)
-    below_1 = go(up_1, "up")
-    over = go(rim, "down")
-    below_0, below_1, over = lax.optimization_barrier((below_0, below_1, over))
-    g0, g1, s0, s1 = call(
+    below = [
+        go(
+            call(functools.partial(send_body, c), piece, [SMEM] + [VMEM] * 2, 8, 1 << 20, 2 << 20)(
+                above, obj, right[c]
+            ),
+            "up",
+        )
+        for c in (0, 1)
+    ]
+    rims = call(rim_body, [(2, 8, W)] * 2, [VMEM] * 4, 8, 1 << 16, 2 << 20)(obj, left, *right)
+    under, over = go(rims[0], "up"), go(rims[1], "down")
+    g0, g1, s0, s1, k0, k1 = call(
         main_body,
-        [piece] * 4,
+        [piece] * 6,
         [SMEM, SMEM] + [VMEM] * 17,
         16,
         5 << 30,
         12 << 20,
         [pltpu.VMEM((4, 2, W, W), f32)],
-    )(offs, live, obj, *right, below_0, below_1, probe, probe_b, probe_c, meas, *tabs)
+    )(offs, counts, obj, *right, *below, probe, probe_b, probe_c, meas, *tabs)
     p1 = go(g1, "swap")
     m0 = go(s0, "right")
     p0 = go(g0, "swap")
     m1 = go(s1, "right")
     b0, b1 = go(g0, "down"), go(g1, "down")
-    base = call(prior_body, whole, [SMEM, SMEM] + [VMEM] * 9, 16, 1 << 28, 16 << 20)(
-        gram, offs, obj, *right, left, over, below_0, below_1, g0, g1
+    base = call(prior_body, whole, [SMEM, SMEM] + [VMEM] * 8, 16, 1 << 28, 16 << 20)(
+        filt, offs, obj, *right, left, over, under, k0, k1
     )
     n1 = go(call(spill_body, piece, [SMEM, VMEM], 8, 1 << 18, 1 << 19)(offs, p1), "right")
     n0 = go(m0, "swap")

time: 83.9 us -> 77 us (0.918)
  the two profiles are of different devices: /device:TPU:97 before, /device:TPU:8 now
where the time goes in v1:
time: 77 us; the launch traced here: 75.7 us
  waiting for transfers between devices  30.8 us (40%)
  starting transfers between devices  21 us (27%)
  Pallas kernels  19.4 us (25%)
  local copies, waits for them, and re-layouts  3.29 us (4%)
  between operations  1.11 us (1%)
    ppermute x22, waiting for transfers between devices, go(): return lax.ppermute(value, axes, ring[where])  30.8 us
    ppermute x22, starting transfers between devices, go(): return lax.ppermute(value, axes, ring[where])  21 us
    pallas_call x1, Pallas kernels, local(): call(main_body, [piece] * 6, [SMEM, SMEM] + [VMEM] * 17, 16, 5 << 30, 12...  7.12 us
    pallas_call x1, Pallas kernels, local(): call(prior_body, whole, [SMEM, SMEM] + [VMEM] * 8, 16, 1 << 28, 16 << 20)  4.68 us
    pallas_call x1, Pallas kernels, local(): call(mid_body, whole, [SMEM, SMEM] + [VMEM] * 11, 12, 1 << 24, 10 << 20)  3.03 us
    pallas_call x1, Pallas kernels, local(): call(final_body, whole, [any_space, VMEM, VMEM], 8, 1 << 18, 2 << 20, [pl...  1.8 us
  transfers between devices with their start and end apart: 22, of which 10 were waited for; matrix products, arithmetic and copies ran while one was open for 3% of the time, Pallas kernels for 23%

profile of v1, /device:TPU:8, one launch (start us, length us, event | category | flops | bytes accessed | tf_op | source)
XLA Modules:
  0.0 75.7 jit_solution(13870986013602028400)
XLA Ops:
  0.0 1.2 %constant_dynamic-slice_fusion = f32[1,2,256,256]{3,2,1,0:T(8,128)S(1)} fusion(f32[2,2,256,256]{3,2,1,0:T(8,128)} %probe_a.1, s32[]{:T(128)S(6)} %select_n.3), kind=kLoop, calls=%fused_computation.2 | loop fusion | bytes 1048580 | tf_op jit(solution)/shard_map/dynamic_slice | solution.py:375
  1.2 1.6 %collective-permute-start.8 = (f32[1,2,256,256]{3,2,1,0:T(8,128)S(1)}, f32[1,2,256,256]{3,2,1,0:T(8,128)S(1)}, u32[]{:S(2)}, u32[]{:S(2)}) collective-permute-start(f32[1,2,256,256]{3,2,1,0:T(8,128)S(1)} %constant_dynamic-slice_fusion), channel_id=1, source_target_pairs={{0,1},{1,0},{2,3},{3,2},{4,5},{5,4},{6,7},{7,6},{8,9},{9,8},{10,11... | collective-permute-start | bytes 1572872 | tf_op jit(solution)/shard_map/ppermute | solution.py:364
  2.8 1.0 %slice_bitcast_fusion.1 = f32[256,256]{1,0:T(8,128)S(1)} fusion(f32[2,256,1024]{2,1,0:T(8,128)} %obj.9), kind=kLoop, calls=%fused_computation.1 | loop fusion | bytes 524288 | tf_op jit(solution)/shard_map/squeeze | solution.py:372
  3.8 0.8 %collective-permute-start.1 = (f32[256,256]{1,0:T(8,128)S(1)}, f32[256,256]{1,0:T(8,128)S(1)}, u32[]{:S(2)}, u32[]{:S(2)}) collective-permute-start(f32[256,256]{1,0:T(8,128)S(1)} %slice_bitcast_fusion.1), channel_id=1, source_target_pairs={{0,15},{1,14},{2,0},{3,1},{4,2},{5,3},{6,4},{7,5},{8,7},{9,6},{10,... | collective-permute-start | bytes 786440 | tf_op jit(solution)/shard_map/ppermute | solution.py:364
  4.6 1.0 %slice_bitcast_fusion = f32[256,256]{1,0:T(8,128)S(1)} fusion(f32[2,256,1024]{2,1,0:T(8,128)} %obj.9), kind=kLoop, calls=%fused_computation | loop fusion | bytes 524288 | tf_op jit(solution)/shard_map/squeeze | solution.py:373
  5.5 4.4 %collective-permute-start.2 = (f32[256,256]{1,0:T(8,128)S(1)}, f32[256,256]{1,0:T(8,128)S(1)}, u32[]{:S(2)}, u32[]{:S(2)}) collective-permute-start(f32[256,256]{1,0:T(8,128)S(1)} %slice_bitcast_fusion), channel_id=1, source_target_pairs={{0,15},{1,14},{2,0},{3,1},{4,2},{5,3},{6,4},{7,5},{8,7},{9,6},{10,... | collective-permute-start | bytes 786440 | tf_op jit(solution)/shard_map/ppermute | solution.py:364
  9.9 5.1 %collective-permute-done.8.probe_b = f32[1,2,256,256]{3,2,1,0:T(8,128)S(1)} collective-permute-done((f32[1,2,256,256]{3,2,1,0:T(8,128)S(1)}, f32[1,2,256,256]{3,2,1,0:T(8,128)S(1)}, u32[]{:S(2)}, u32[]{:S(2)}) %collective-permute-start.8) | collective-permute-done | bytes 524320 | tf_op jit(solution)/shard_map/ppermute | solution.py:364
  15.0 0.5 collective-permute-start
  15.5 6.7 %collective-permute-done.above = s32[2,2]{1,0:T(2,128)S(1)} collective-permute-done((s32[2,2]{1,0:T(2,128)S(1)}, s32[2,2]{1,0:T(2,128)S(1)}, u32[]{:S(2)}, u32[]{:S(2)}) %collective-permute-start) | collective-permute-done | bytes 48 | tf_op jit(solution)/shard_map/ppermute | solution.py:364
  22.2 0.6 shard_map.137
  22.9 0.0 copy-start.5
  22.9 0.0 copy-start.6
  22.9 0.0 copy-start.7
  22.9 0.0 copy-start.8
  22.9 0.0 copy-start.9
  22.9 0.0 copy-start.10
  23.0 0.0 copy-start.11
  23.0 0.0 copy-start.12
  23.0 0.2 collective-permute-start.6
  23.1 0.6 shard_map.138
  23.8 1.6 %collective-permute-start.7 = (f32[256,256]{1,0:T(8,128)S(1)}, f32[256,256]{1,0:T(8,128)S(1)}, u32[]{:S(2)}, u32[]{:S(2)}) collective-permute-start(f32[256,256]{1,0:T(8,128)S(1)} %shard_map.138), channel_id=1, source_target_pairs={{0,240},{1,241},{2,242},{3,243},{4,244},{5,245},{6,246},{7,247},{8... | collective-permute-start | bytes 786440 | tf_op jit(solution)/shard_map/ppermute | solution.py:364
  25.4 1.7 %collective-permute-start.3 = (f32[2,256,128]{2,1,0:T(8,128)S(1)}, f32[2,256,128]{2,1,0:T(8,128)S(1)}, u32[]{:S(2)}, u32[]{:S(2)}) collective-permute-start(f32[2,256,128]{2,1,0:T(8,128)S(1)} %slice.11), channel_id=1, source_target_pairs={{0,2},{1,3},{2,4},{3,5},{4,6},{5,7},{6,9},{7,8},{8,10},{9,11},{10,... | collective-permute-start | bytes 786440 | tf_op jit(solution)/shard_map/ppermute | solution.py:364
  27.7 0.7 shard_map.139.meas
  28.4 1.4 %collective-permute-done.7.below_1 = f32[256,256]{1,0:T(8,128)S(1)} collective-permute-done((f32[256,256]{1,0:T(8,128)S(1)}, f32[256,256]{1,0:T(8,128)S(1)}, u32[]{:S(2)}, u32[]{:S(2)}) %collective-permute-start.7) | collective-permute-done | bytes 262176 | tf_op jit(solution)/shard_map/ppermute | solution.py:364
  29.9 7.1 %shard_map.140 = (f32[256,256]{1,0:T(8,128)S(1)}, f32[256,256]{1,0:T(8,128)S(1)}, f32[256,256]{1,0:T(8,128)S(1)}, f32[256,256]{1,0:T(8,128)S(1)}, f32[256,256]{1,0:T(8,128)S(1)}, /*index=5*/f32[256,256]{1,0:T(8,128)S(1)}) custom-call(s32[2,2]{1,0:T(2,128)S(1)} %bitcast.7, s32[1,1]{1,0:T(1,128)S(6)} %copy.17.counts, f32[2,256,1024]{2,1,0:T(8,128)S(1)} %copy-done, ...), custom_call_target="tpu_custom_call" | custom-call | flops 5368709120 | bytes 12582912 | tf_op jit(solution)/shard_map/pallas_call | solution.py:392
  37.0 1.7 %collective-permute-start.12 = (f32[256,256]{1,0:T(8,128)S(1)}, f32[256,256]{1,0:T(8,128)S(1)}, u32[]{:S(2)}, u32[]{:S(2)}) collective-permute-start(f32[256,256]{1,0:T(8,128)S(1)} %get-tuple-element.19), channel_id=1, source_target_pairs={{0,2},{1,3},{2,4},{3,5},{4,6},{5,7},{6,9},{7,8},{8,10},{9,11},{10,... | collective-permute-start | bytes 786440 | tf_op jit(solution)/shard_map/ppermute | solution.py:364
  38.7 1.5 %collective-permute-start.11 = (f32[256,256]{1,0:T(8,128)S(1)}, f32[256,256]{1,0:T(8,128)S(1)}, u32[]{:S(2)}, u32[]{:S(2)}) collective-permute-start(f32[256,256]{1,0:T(8,128)S(1)} %get-tuple-element.18), channel_id=1, source_target_pairs={{0,1},{1,0},{2,3},{3,2},{4,5},{5,4},{6,7},{7,6},{8,9},{9,8},{10,11... | collective-permute-start | bytes 786440 | tf_op jit(solution)/shard_map/ppermute | solution.py:364
  40.2 0.5 collective-permute-start.10
  40.8 0.0 collective-permute-start.4
  40.8 1.5 %collective-permute-start.13 = (f32[256,256]{1,0:T(8,128)S(1)}, f32[256,256]{1,0:T(8,128)S(1)}, u32[]{:S(2)}, u32[]{:S(2)}) collective-permute-start(f32[256,256]{1,0:T(8,128)S(1)} %get-tuple-element.20), channel_id=1, source_target_pairs={{0,2},{1,3},{2,4},{3,5},{4,6},{5,7},{6,9},{7,8},{8,10},{9,11},{10,... | collective-permute-start | bytes 786440 | tf_op jit(solution)/shard_map/ppermute | solution.py:364
  42.3 4.0 %collective-permute-done.12.refs_2_.one = f32[256,256]{1,0:T(8,128)S(1)} collective-permute-done((f32[256,256]{1,0:T(8,128)S(1)}, f32[256,256]{1,0:T(8,128)S(1)}, u32[]{:S(2)}, u32[]{:S(2)}) %collective-permute-start.12) | collective-permute-done | bytes 262176 | tf_op jit(solution)/shard_map/ppermute | solution.py:364
  46.3 1.5 %collective-permute-start.14 = (f32[256,256]{1,0:T(8,128)S(1)}, f32[256,256]{1,0:T(8,128)S(1)}, u32[]{:S(2)}, u32[]{:S(2)}) collective-permute-start(f32[256,256]{1,0:T(8,128)S(1)} %collective-permute-done.12.refs_2_.one), channel_id=1, source_target_pairs={{0,1},{1,0},{2,3},{3,2},{4,5},{5,4},{6,7},{7,6},{8,9},{9,8},{10,11... | collective-permute-start | bytes 786440 | tf_op jit(solution)/shard_map/ppermute | solution.py:364
  47.8 0.1 collective-permute-done.11.grad.refs_1_
  47.9 0.6 shard_map.142
  48.5 1.6 %collective-permute-start.15 = (f32[256,256]{1,0:T(8,128)S(1)}, f32[256,256]{1,0:T(8,128)S(1)}, u32[]{:S(2)}, u32[]{:S(2)}) collective-permute-start(f32[256,256]{1,0:T(8,128)S(1)} %shard_map.142), channel_id=1, source_target_pairs={{0,2},{1,3},{2,4},{3,5},{4,6},{5,7},{6,9},{7,8},{8,10},{9,11},{10,... | collective-permute-start | bytes 786440 | tf_op jit(solution)/shard_map/ppermute | solution.py:364
  50.0 3.4 %collective-permute-done.10.refs_0_ = f32[256,256]{1,0:T(8,128)S(1)} collective-permute-done((f32[256,256]{1,0:T(8,128)S(1)}, f32[256,256]{1,0:T(8,128)S(1)}, u32[]{:S(2)}, u32[]{:S(2)}) %collective-permute-start.10) | collective-permute-done | bytes 262176 | tf_op jit(solution)/shard_map/ppermute | solution.py:364
  53.5 2.0 %collective-permute-start.5 = (f32[2,8,256]{2,1,0:T(8,128)S(1)}, f32[2,8,256]{2,1,0:T(8,128)S(1)}, u32[]{:S(2)}, u32[]{:S(2)}) collective-permute-start(f32[2,8,256]{2,1,0:T(8,128)S(1)} %get-tuple-element.14), channel_id=1, source_target_pairs={{0,240},{1,241},{2,242},{3,243},{4,244},{5,245},{6,246},{7,247},{8... | collective-permute-start | bytes 49160 | tf_op jit(solution)/shard_map/ppermute | solution.py:364
  55.5 2.8 %collective-permute-done.14.refs_4_.two = f32[256,256]{1,0:T(8,128)S(1)} collective-permute-done((f32[256,256]{1,0:T(8,128)S(1)}, f32[256,256]{1,0:T(8,128)S(1)}, u32[]{:S(2)}, u32[]{:S(2)}) %collective-permute-start.14) | collective-permute-done | bytes 262176 | tf_op jit(solution)/shard_map/ppermute | solution.py:364
  58.3 0.1 shard_map.144
  58.4 0.1 shard_map.145
  58.6 0.0 collective-permute-start.20
  58.6 0.0 collective-permute-start.21
  58.6 4.7 %shard_map.141.base = f32[2,256,1024]{2,1,0:T(8,128)S(1)} custom-call(f32[4,16]{1,0:T(4,128)S(1)} %bitcast.11, s32[2,2]{1,0:T(2,128)S(1)} %bitcast.9, f32[2,256,1024]{2,1,0:T(8,128)S(1)} %copy-done, f32[256,256]{1,0:T(8,128)S(1)} %collective-permute-done.1.right_0.right, f32[256,256]{1,0:T(8,128)S(1)} %collective-permute-done.2.right_1.right, ...), custom_call_target="tpu_custom_call" | custom-call | flops 268435456 | bytes 16777216 | tf_op jit(solution)/shard_map/pallas_call | solution.py:406
  63.3 1.9 %collective-permute-done.18.refs_8_ = f32[256,256]{1,0:T(8,128)S(1)} collective-permute-done((f32[256,256]{1,0:T(8,128)S(1)}, f32[256,256]{1,0:T(8,128)S(1)}, u32[]{:S(2)}, u32[]{:S(2)}) %collective-permute-start.18) | collective-permute-done | bytes 262176 | tf_op jit(solution)/shard_map/ppermute | solution.py:364
  65.3 2.8 %collective-permute-done.19.refs_9_ = f32[256,256]{1,0:T(8,128)S(1)} collective-permute-done((f32[256,256]{1,0:T(8,128)S(1)}, f32[256,256]{1,0:T(8,128)S(1)}, u32[]{:S(2)}, u32[]{:S(2)}) %collective-permute-start.19) | collective-permute-done | bytes 262176 | tf_op jit(solution)/shard_map/ppermute | solution.py:364
  68.1 3.0 %shard_map.143.mid = f32[2,256,1024]{2,1,0:T(8,128)} custom-call(s32[2,2]{1,0:T(2,128)S(1)} %bitcast.10, s32[2,2]{1,0:T(2,128)S(1)} %collective-permute-done.above, f32[2,256,1024]{2,1,0:T(8,128)S(1)} %shard_map.141.base, f32[256,256]{1,0:T(8,128)S(1)} %collective-permute-done.10.refs_0_, f32[256,256]{1,0:T(8,128)S(1)} %collective-permute-done.11.grad.refs_1_, ...), custom_call_target="tpu_custom_call" | custom-call | flops 16777216 | bytes 10485760 | tf_op jit(solution)/shard_map/pallas_call | solution.py:416
  71.1 2.6 %collective-permute-done.21.corner_1 = f32[256,256]{1,0:T(8,128)S(1)} collective-permute-done((f32[256,256]{1,0:T(8,128)S(1)}, f32[256,256]{1,0:T(8,128)S(1)}, u32[]{:S(2)}, u32[]{:S(2)}) %collective-permute-start.21) | collective-permute-done | bytes 262176 | tf_op jit(solution)/shard_map/ppermute | solution.py:364
  73.7 1.8 %shard_map.146 = f32[2,256,1024]{2,1,0:T(8,128)} custom-call(f32[2,256,1024]{2,1,0:T(8,128)} %shard_map.143.mid, f32[256,256]{1,0:T(8,128)S(1)} %collective-permute-done.20.corner_0, f32[256,256]{1,0:T(8,128)S(1)} %collective-permute-done.21.corner_1), custom_call_target="tpu_custom_call", output_to_operand_aliasing={{}: (0, {})} | custom-call | flops 262144 | bytes 2097152 | tf_op jit(solution)/shard_map/pallas_call | solution.py:420
  (37 shorter events, 0.1 us)
Async XLA Ops:
  0.0 22.2 %copy-start = (f32[2,256,1024]{2,1,0:T(8,128)S(1)}, f32[2,256,1024]{2,1,0:T(8,128)}, u32[]{:S(2)}) copy-start(f32[2,256,1024]{2,1,0:T(8,128)} %obj.9) | copy-start | bytes 6291460
  0.0 15.0 %copy-start.3 = (s32[1,1,2,2]{3,2,1,0:T(2,128)S(1)}, s32[1,1,2,2]{3,2,1,0:T(2,128)}, u32[]{:S(2)}) copy-start(s32[1,1,2,2]{3,2,1,0:T(2,128)} %param.17) | copy-start | bytes 52
  1.2 13.8 %collective-permute-start.8 = (f32[1,2,256,256]{3,2,1,0:T(8,128)S(1)}, f32[1,2,256,256]{3,2,1,0:T(8,128)S(1)}, u32[]{:S(2)}, u32[]{:S(2)}) collective-permute-start(f32[1,2,256,256]{3,2,1,0:T(8,128)S(1)} %constant_dynamic-slice_fusion), channel_id=1, source_target_pairs={{0,1},{1,0},{2,3},{3,2},{4,5},{5,4},{6,7},{7,6},{8,9},{9,8},{10,11... | collective-permute-start | bytes 1572872 | tf_op jit(solution)/shard_map/ppermute | solution.py:364
  3.8 18.4 %collective-permute-start.1 = (f32[256,256]{1,0:T(8,128)S(1)}, f32[256,256]{1,0:T(8,128)S(1)}, u32[]{:S(2)}, u32[]{:S(2)}) collective-permute-start(f32[256,256]{1,0:T(8,128)S(1)} %slice_bitcast_fusion.1), channel_id=1, source_target_pairs={{0,15},{1,14},{2,0},{3,1},{4,2},{5,3},{6,4},{7,5},{8,7},{9,6},{10,... | collective-permute-start | bytes 786440 | tf_op jit(solution)/shard_map/ppermute | solution.py:364
  5.5 17.6 %collective-permute-start.2 = (f32[256,256]{1,0:T(8,128)S(1)}, f32[256,256]{1,0:T(8,128)S(1)}, u32[]{:S(2)}, u32[]{:S(2)}) collective-permute-start(f32[256,256]{1,0:T(8,128)S(1)} %slice_bitcast_fusion), channel_id=1, source_target_pairs={{0,15},{1,14},{2,0},{3,1},{4,2},{5,3},{6,4},{7,5},{8,7},{9,6},{10,... | collective-permute-start | bytes 786440 | tf_op jit(solution)/shard_map/ppermute | solution.py:364
  15.0 14.8 %collective-permute-start.9 = (f32[1,2,256,256]{3,2,1,0:T(8,128)S(1)}, f32[1,2,256,256]{3,2,1,0:T(8,128)S(1)}, u32[]{:S(2)}, u32[]{:S(2)}) collective-permute-start(f32[1,2,256,256]{3,2,1,0:T(8,128)S(1)} %collective-permute-done.8.probe_b), channel_id=1, source_target_pairs={{0,16},{1,17},{2,18},{3,19},{4,20},{5,21},{6,22},{7,23},{8,24},{9,... | collective-permute-start | bytes 1572872 | tf_op jit(solution)/shard_map/ppermute | solution.py:364
  15.0 7.2 %collective-permute-start = (s32[2,2]{1,0:T(2,128)S(1)}, s32[2,2]{1,0:T(2,128)S(1)}, u32[]{:S(2)}, u32[]{:S(2)}) collective-permute-start(s32[2,2]{1,0:T(2,128)S(1)} %bitcast.6), channel_id=1, source_target_pairs={{0,16},{1,17},{2,18},{3,19},{4,20},{5,21},{6,22},{7,23},{8,24},{9,... | collective-permute-start | bytes 56 | tf_op jit(solution)/shard_map/ppermute | solution.py:364
  22.9 4.9 %copy-start.1 = (f32[1,1,2,256,256]{4,3,2,1,0:T(8,128)S(1)}, f32[1,1,2,256,256]{4,3,2,1,0:T(8,128)}, u32[]{:S(2)}) copy-start(f32[1,1,2,256,256]{4,3,2,1,0:T(8,128)} %meas.1) | copy-start | bytes 1572868
  22.9 7.0 %copy-start.2 = (f32[2,2,256,256]{3,2,1,0:T(8,128)S(1)}, f32[2,2,256,256]{3,2,1,0:T(8,128)}, u32[]{:S(2)}) copy-start(f32[2,2,256,256]{3,2,1,0:T(8,128)} %probe_a.1) | copy-start | bytes 3145732
  22.9 7.0 %copy-start.5 = (bf16[256,256]{1,0:T(8,128)(2,1)S(1)}, bf16[256,256]{1,0:T(8,128)(2,1)}, u32[]{:S(2)}) copy-start(bf16[256,256]{1,0:T(8,128)(2,1)} %constant.28.clone.refs_0_) | copy-start | bytes 393220
  22.9 7.0 %copy-start.6 = (bf16[256,256]{1,0:T(8,128)(2,1)S(1)}, bf16[256,256]{1,0:T(8,128)(2,1)}, u32[]{:S(2)}) copy-start(bf16[256,256]{1,0:T(8,128)(2,1)} %constant.29.clone.refs_1_) | copy-start | bytes 393220
  22.9 7.0 %copy-start.7 = (bf16[256,256]{1,0:T(8,128)(2,1)S(1)}, bf16[256,256]{1,0:T(8,128)(2,1)}, u32[]{:S(2)}) copy-start(bf16[256,256]{1,0:T(8,128)(2,1)} %constant.30.clone.refs_2_) | copy-start | bytes 393220
  22.9 6.9 %copy-start.8 = (bf16[256,256]{1,0:T(8,128)(2,1)S(1)}, bf16[256,256]{1,0:T(8,128)(2,1)}, u32[]{:S(2)}) copy-start(bf16[256,256]{1,0:T(8,128)(2,1)} %constant.31.clone.refs_3_) | copy-start | bytes 393220
  22.9 6.9 %copy-start.9 = (bf16[256,256]{1,0:T(8,128)(2,1)S(1)}, bf16[256,256]{1,0:T(8,128)(2,1)}, u32[]{:S(2)}) copy-start(bf16[256,256]{1,0:T(8,128)(2,1)} %constant.32.clone.refs_4_) | copy-start | bytes 393220
  22.9 6.9 %copy-start.10 = (bf16[256,256]{1,0:T(8,128)(2,1)S(1)}, bf16[256,256]{1,0:T(8,128)(2,1)}, u32[]{:S(2)}) copy-start(bf16[256,256]{1,0:T(8,128)(2,1)} %constant.33.clone.refs_5_) | copy-start | bytes 393220
  23.0 6.9 %copy-start.11 = (bf16[256,256]{1,0:T(8,128)(2,1)S(1)}, bf16[256,256]{1,0:T(8,128)(2,1)}, u32[]{:S(2)}) copy-start(bf16[256,256]{1,0:T(8,128)(2,1)} %constant.34.clone.refs_6_) | copy-start | bytes 393220
  23.0 6.9 %copy-start.12 = (bf16[256,256]{1,0:T(8,128)(2,1)S(1)}, bf16[256,256]{1,0:T(8,128)(2,1)}, u32[]{:S(2)}) copy-start(bf16[256,256]{1,0:T(8,128)(2,1)} %constant.35.clone.refs_7_) | copy-start | bytes 393220
  23.0 5.4 %collective-permute-start.6 = (f32[256,256]{1,0:T(8,128)S(1)}, f32[256,256]{1,0:T(8,128)S(1)}, u32[]{:S(2)}, u32[]{:S(2)}) collective-permute-start(f32[256,256]{1,0:T(8,128)S(1)} %shard_map.137), channel_id=1, source_target_pairs={{0,240},{1,241},{2,242},{3,243},{4,244},{5,245},{6,246},{7,247},{8... | collective-permute-start | bytes 786440 | tf_op jit(solution)/shard_map/ppermute | solution.py:364
  23.8 6.1 %collective-permute-start.7 = (f32[256,256]{1,0:T(8,128)S(1)}, f32[256,256]{1,0:T(8,128)S(1)}, u32[]{:S(2)}, u32[]{:S(2)}) collective-permute-start(f32[256,256]{1,0:T(8,128)S(1)} %shard_map.138), channel_id=1, source_target_pairs={{0,240},{1,241},{2,242},{3,243},{4,244},{5,245},{6,246},{7,247},{8... | collective-permute-start | bytes 786440 | tf_op jit(solution)/shard_map/ppermute | solution.py:364
  25.4 15.3 %collective-permute-start.3 = (f32[2,256,128]{2,1,0:T(8,128)S(1)}, f32[2,256,128]{2,1,0:T(8,128)S(1)}, u32[]{:S(2)}, u32[]{:S(2)}) collective-permute-start(f32[2,256,128]{2,1,0:T(8,128)S(1)} %slice.11), channel_id=1, source_target_pairs={{0,2},{1,3},{2,4},{3,5},{4,6},{5,7},{6,9},{7,8},{8,10},{9,11},{10,... | collective-permute-start | bytes 786440 | tf_op jit(solution)/shard_map/ppermute | solution.py:364
  37.0 9.3 %collective-permute-start.12 = (f32[256,256]{1,0:T(8,128)S(1)}, f32[256,256]{1,0:T(8,128)S(1)}, u32[]{:S(2)}, u32[]{:S(2)}) collective-permute-start(f32[256,256]{1,0:T(8,128)S(1)} %get-tuple-element.19), channel_id=1, source_target_pairs={{0,2},{1,3},{2,4},{3,5},{4,6},{5,7},{6,9},{7,8},{8,10},{9,11},{10,... | collective-permute-start | bytes 786440 | tf_op jit(solution)/shard_map/ppermute | solution.py:364
  38.7 9.2 %collective-permute-start.11 = (f32[256,256]{1,0:T(8,128)S(1)}, f32[256,256]{1,0:T(8,128)S(1)}, u32[]{:S(2)}, u32[]{:S(2)}) collective-permute-start(f32[256,256]{1,0:T(8,128)S(1)} %get-tuple-element.18), channel_id=1, source_target_pairs={{0,1},{1,0},{2,3},{3,2},{4,5},{5,4},{6,7},{7,6},{8,9},{9,8},{10,11... | collective-permute-start | bytes 786440 | tf_op jit(solution)/shard_map/ppermute | solution.py:364
  40.2 18.5 %copy-start.4 = (f32[16,4]{0,1:T(4,128)S(1)}, f32[16,4]{0,1:T(4,128)}, u32[]{:S(2)}) copy-start(f32[16,4]{0,1:T(4,128)} %param.19) | copy-start | bytes 772
  40.2 13.3 %collective-permute-start.10 = (f32[256,256]{1,0:T(8,128)S(1)}, f32[256,256]{1,0:T(8,128)S(1)}, u32[]{:S(2)}, u32[]{:S(2)}) collective-permute-start(f32[256,256]{1,0:T(8,128)S(1)} %get-tuple-element.17), channel_id=1, source_target_pairs={{0,1},{1,0},{2,3},{3,2},{4,5},{5,4},{6,7},{7,6},{8,9},{9,8},{10,11... | collective-permute-start | bytes 786440 | tf_op jit(solution)/shard_map/ppermute | solution.py:364
  40.8 9.3 %collective-permute-start.4 = (f32[2,8,256]{2,1,0:T(8,128)S(1)}, f32[2,8,256]{2,1,0:T(8,128)S(1)}, u32[]{:S(2)}, u32[]{:S(2)}) collective-permute-start(f32[2,8,256]{2,1,0:T(8,128)S(1)} %get-tuple-element.13), channel_id=1, source_target_pairs={{0,16},{1,17},{2,18},{3,19},{4,20},{5,21},{6,22},{7,23},{8,24},{9,... | collective-permute-start | bytes 49160 | tf_op jit(solution)/shard_map/ppermute | solution.py:364
  40.8 14.7 %collective-permute-start.13 = (f32[256,256]{1,0:T(8,128)S(1)}, f32[256,256]{1,0:T(8,128)S(1)}, u32[]{:S(2)}, u32[]{:S(2)}) collective-permute-start(f32[256,256]{1,0:T(8,128)S(1)} %get-tuple-element.20), channel_id=1, source_target_pairs={{0,2},{1,3},{2,4},{3,5},{4,6},{5,7},{6,9},{7,8},{8,10},{9,11},{10,... | collective-permute-start | bytes 786440 | tf_op jit(solution)/shard_map/ppermute | solution.py:364
  46.3 12.0 %collective-permute-start.14 = (f32[256,256]{1,0:T(8,128)S(1)}, f32[256,256]{1,0:T(8,128)S(1)}, u32[]{:S(2)}, u32[]{:S(2)}) collective-permute-start(f32[256,256]{1,0:T(8,128)S(1)} %collective-permute-done.12.refs_2_.one), channel_id=1, source_target_pairs={{0,1},{1,0},{2,3},{3,2},{4,5},{5,4},{6,7},{7,6},{8,9},{9,8},{10,11... | collective-permute-start | bytes 786440 | tf_op jit(solution)/shard_map/ppermute | solution.py:364
  48.5 9.8 %collective-permute-start.15 = (f32[256,256]{1,0:T(8,128)S(1)}, f32[256,256]{1,0:T(8,128)S(1)}, u32[]{:S(2)}, u32[]{:S(2)}) collective-permute-start(f32[256,256]{1,0:T(8,128)S(1)} %shard_map.142), channel_id=1, source_target_pairs={{0,2},{1,3},{2,4},{3,5},{4,6},{5,7},{6,9},{7,8},{8,10},{9,11},{10,... | collective-permute-start | bytes 786440 | tf_op jit(solution)/shard_map/ppermute | solution.py:364
  50.0 8.6 %collective-permute-start.16 = (f32[256,256]{1,0:T(8,128)S(1)}, f32[256,256]{1,0:T(8,128)S(1)}, u32[]{:S(2)}, u32[]{:S(2)}) collective-permute-start(f32[256,256]{1,0:T(8,128)S(1)} %get-tuple-element.17), channel_id=1, source_target_pairs={{0,16},{1,17},{2,18},{3,19},{4,20},{5,21},{6,22},{7,23},{8,24},{9,... | collective-permute-start | bytes 786440 | tf_op jit(solution)/shard_map/ppermute | solution.py:364
  53.5 5.1 %collective-permute-start.5 = (f32[2,8,256]{2,1,0:T(8,128)S(1)}, f32[2,8,256]{2,1,0:T(8,128)S(1)}, u32[]{:S(2)}, u32[]{:S(2)}) collective-permute-start(f32[2,8,256]{2,1,0:T(8,128)S(1)} %get-tuple-element.14), channel_id=1, source_target_pairs={{0,240},{1,241},{2,242},{3,243},{4,244},{5,245},{6,246},{7,247},{8... | collective-permute-start | bytes 49160 | tf_op jit(solution)/shard_map/ppermute | solution.py:364
  55.5 7.9 %collective-permute-start.17 = (f32[256,256]{1,0:T(8,128)S(1)}, f32[256,256]{1,0:T(8,128)S(1)}, u32[]{:S(2)}, u32[]{:S(2)}) collective-permute-start(f32[256,256]{1,0:T(8,128)S(1)} %get-tuple-element.18), channel_id=1, source_target_pairs={{0,16},{1,17},{2,18},{3,19},{4,20},{5,21},{6,22},{7,23},{8,24},{9,... | collective-permute-start | bytes 786440 | tf_op jit(solution)/shard_map/ppermute | solution.py:364
  58.3 7.0 %collective-permute-start.18 = (f32[256,256]{1,0:T(8,128)S(1)}, f32[256,256]{1,0:T(8,128)S(1)}, u32[]{:S(2)}, u32[]{:S(2)}) collective-permute-start(f32[256,256]{1,0:T(8,128)S(1)} %collective-permute-done.10.refs_0_), channel_id=1, source_target_pairs={{0,16},{1,17},{2,18},{3,19},{4,20},{5,21},{6,22},{7,23},{8,24},{9,... | collective-permute-start | bytes 786440 | tf_op jit(solution)/shard_map/ppermute | solution.py:364
  58.3 9.8 %collective-permute-start.19 = (f32[256,256]{1,0:T(8,128)S(1)}, f32[256,256]{1,0:T(8,128)S(1)}, u32[]{:S(2)}, u32[]{:S(2)}) collective-permute-start(f32[256,256]{1,0:T(8,128)S(1)} %collective-permute-done.11.grad.refs_1_), channel_id=1, source_target_pairs={{0,16},{1,17},{2,18},{3,19},{4,20},{5,21},{6,22},{7,23},{8,24},{9,... | collective-permute-start | bytes 786440 | tf_op jit(solution)/shard_map/ppermute | solution.py:364
  58.6 12.6 %collective-permute-start.20 = (f32[256,256]{1,0:T(8,128)S(1)}, f32[256,256]{1,0:T(8,128)S(1)}, u32[]{:S(2)}, u32[]{:S(2)}) collective-permute-start(f32[256,256]{1,0:T(8,128)S(1)} %shard_map.144), channel_id=1, source_target_pairs={{0,16},{1,17},{2,18},{3,19},{4,20},{5,21},{6,22},{7,23},{8,24},{9,... | collective-permute-start | bytes 786440 | tf_op jit(solution)/shard_map/ppermute | solution.py:364
  58.6 15.1 %collective-permute-start.21 = (f32[256,256]{1,0:T(8,128)S(1)}, f32[256,256]{1,0:T(8,128)S(1)}, u32[]{:S(2)}, u32[]{:S(2)}) collective-permute-start(f32[256,256]{1,0:T(8,128)S(1)} %shard_map.145), channel_id=1, source_target_pairs={{0,16},{1,17},{2,18},{3,19},{4,20},{5,21},{6,22},{7,23},{8,24},{9,... | collective-permute-start | bytes 786440 | tf_op jit(solution)/shard_map/ppermute | solution.py:364
